TPU v7x, 512 devices: a whole 4x4x16 slice. The times are simulated.
512 devices in a mesh: dp: 16 (over z_lo, y), ctx: 32 (over z_hi, x, core).
Axes of the slice: x: 4, y: 4, z: 16 (z_hi: 4, z_lo: 4; z = z_hi * 4 + z_lo), core: 2. Of those that a mesh axis runs over, the one named last changes fastest.
Arguments:
- tokens_in: bfloat16 [16, 6144, 2880], P('dp', 'ctx'), may hold values from -6 to 6
- queries: bfloat16 [16, 6144, 2048], P('dp', 'ctx'), may hold values from -20 to 20
- values_in: bfloat16 [16, 6144, 256], P('dp', 'ctx'), may hold values from -6 to 6
- key_weight: bfloat16 [2880, 256], P('dp', 'ctx'), may hold values from -0.109375 to 0.109375
- out_grad: bfloat16 [16, 6144, 2048], P('dp', 'ctx'), may hold values from -6 to 6
- doc_ids: int32 [16, 6144], P('dp'), may hold values from 0 to 15, never falling along the last dimension, each value on 1 to 768 neighbouring positions
Outputs:
- query_grad: bfloat16 [16, 6144, 2048], P('dp', 'ctx')
- value_grad: bfloat16 [16, 6144, 256], P('dp', 'ctx')
- input_grad: bfloat16 [16, 6144, 2880], P('dp', 'ctx')
- key_weight_grad: float32 [2880, 256], P('dp', 'ctx')
Inputs may be any that keep to these rules, and one draw needn't show every extreme that they name: `doc_ids`: ids never fall along a sequence; a document has at most 768 tokens.
All inputs are finite; a program needn't handle non-finite values.
Results may differ from a plain program's by a relative error of at most 0.02.
The roundings to bfloat16 on the way count: a program that leaves them out, or rounds other values in their place, can miss the bound.
Values may be sent and summed in bfloat16 or wider, within the bound.
No kernel may reach another device: no remote copies, remote signals or barrier semaphores. Data moves between devices by JAX's collectives and lax.ppermute only.
A program may use at most 64 MiB of HBM per device.

v0:
```python
import math

import jax
import jax.numpy as jnp
from jax import lax
from jax.sharding import PartitionSpec as P

QUERY_HEAD_COUNT = 32
KEY_VALUE_HEADS = 4
HEAD_SIZE = 64
WINDOW_LENGTH = 128
KEY_FEATURES = 256


rope_base = 150000.0
masked_score = -1e30


def passed_along(array, axis, by):
    peers = lax.axis_size(axis)
    pairs = [(i, i + by) for i in range(peers) if 0 <= i + by < peers]
    return lax.ppermute(array, axis, pairs)


def rope_tables(positions):
    half_dim = HEAD_SIZE // 2
    exponent = jnp.arange(half_dim, dtype=jnp.float32) * (-2.0 / HEAD_SIZE)
    inverse_freq = jnp.power(jnp.float32(rope_base), exponent)
    angles = positions.astype(jnp.float32)[:, None] * inverse_freq[None, :]
    return (jnp.cos(angles)[:, None, :], jnp.sin(angles)[:, None, :])


def apply_rotary(tensor, cosine_table, sine_table):
    half_dim = HEAD_SIZE // 2
    first_half = tensor[..., :half_dim]
    second_half = tensor[..., half_dim:]
    return jnp.concatenate(
        [
            first_half * cosine_table - second_half * sine_table,
            second_half * cosine_table + first_half * sine_table,
        ],
        axis=-1,
    )


def invert_rotary(tensor, cosine_table, sine_table):
    half_dim = HEAD_SIZE // 2
    first_half = tensor[..., :half_dim]
    second_half = tensor[..., half_dim:]
    return jnp.concatenate(
        [
            first_half * cosine_table + second_half * sine_table,
            second_half * cosine_table - first_half * sine_table,
        ],
        axis=-1,
    )


def band_block(
    query_row_tensor, gradient_rows, key_row_tensor, value_row_tensor, query_docs, key_docs
):
    row_number_total = query_row_tensor.shape[0]
    key_window_span = key_row_tensor.shape[0]
    query_group_width = QUERY_HEAD_COUNT // KEY_VALUE_HEADS
    score_scale = HEAD_SIZE ** (-0.5)
    query_head_tensor = query_row_tensor.reshape(
        row_number_total, KEY_VALUE_HEADS, query_group_width, HEAD_SIZE
    )
    gradient_heads = gradient_rows.reshape(
        row_number_total, KEY_VALUE_HEADS, query_group_width, HEAD_SIZE
    )
    key_head_tensor = key_row_tensor.reshape(key_window_span, KEY_VALUE_HEADS, HEAD_SIZE)
    value_head_tensor = value_row_tensor.reshape(key_window_span, KEY_VALUE_HEADS, HEAD_SIZE)
    scores = (
        jnp.einsum(
            "rkgd,ckd->kgrc", query_head_tensor, key_head_tensor, preferred_element_type=jnp.float32
        )
        * score_scale
    )
    distance = (
        jnp.arange(row_number_total, dtype=jnp.int32)[:, None]
        + WINDOW_LENGTH
        - jnp.arange(key_window_span, dtype=jnp.int32)[None, :]
    )
    allowed = (
        (distance >= 0) & (distance <= WINDOW_LENGTH) & (query_docs[:, None] == key_docs[None, :])
    )
    scores = jnp.where(allowed[None, None], scores, masked_score)
    row_max = jnp.max(scores, axis=-1, keepdims=True)
    weights = jnp.exp(scores - row_max)
    prob_rows = weights / jnp.sum(weights, axis=-1, keepdims=True)
    probs_low = prob_rows.astype(jnp.bfloat16)
    attn_out = jnp.einsum(
        "kgrc,ckd->rkgd", probs_low, value_head_tensor, preferred_element_type=jnp.float32
    )
    row_delta = jnp.sum(gradient_heads.astype(jnp.float32) * attn_out, axis=-1)
    value_part = jnp.einsum(
        "kgrc,rkgd->ckd", probs_low, gradient_heads, preferred_element_type=jnp.float32
    )
    prob_grad = jnp.einsum(
        "rkgd,ckd->kgrc", gradient_heads, value_head_tensor, preferred_element_type=jnp.float32
    )
    score_grad = prob_rows * (prob_grad - jnp.transpose(row_delta, (1, 2, 0))[..., None])
    score_low = score_grad.astype(jnp.bfloat16)
    query_part = (
        jnp.einsum("kgrc,ckd->rkgd", score_low, key_head_tensor, preferred_element_type=jnp.float32)
        * score_scale
    )
    key_part = (
        jnp.einsum(
            "kgrc,rkgd->ckd", score_low, query_head_tensor, preferred_element_type=jnp.float32
        )
        * score_scale
    )
    return (
        query_part.reshape(row_number_total, QUERY_HEAD_COUNT * HEAD_SIZE),
        key_part.reshape(key_window_span, KEY_FEATURES),
        value_part.reshape(key_window_span, KEY_FEATURES),
    )


def per_device(tokens_in, queries, values_in, key_weight, out_grad, doc_ids):
    row_overall_count = tokens_in.shape[1]
    position = lax.axis_index("ctx")
    columns = lax.all_gather(key_weight, "ctx", axis=1, tiled=True)
    full_weight = lax.all_gather(columns, "dp", axis=0, tiled=True)
    inputs = tokens_in[0]
    query_row_tensor = queries[0]
    gradient_rows = out_grad[0]
    value_row_tensor = values_in[0]
    first_row = position * row_overall_count
    positions = first_row + jnp.arange(row_overall_count, dtype=jnp.int32)
    cosine_table, sine_table = rope_tables(positions)
    key_linear_output = jnp.dot(inputs, full_weight, preferred_element_type=jnp.float32)
    keys_reduced_precision = (
        apply_rotary(
            key_linear_output.reshape(row_overall_count, KEY_VALUE_HEADS, HEAD_SIZE),
            cosine_table,
            sine_table,
        )
        .reshape(row_overall_count, KEY_FEATURES)
        .astype(jnp.bfloat16)
    )
    prior_keys, prior_values = passed_along(
        (
            keys_reduced_precision[row_overall_count - WINDOW_LENGTH :],
            value_row_tensor[row_overall_count - WINDOW_LENGTH :],
        ),
        "ctx",
        1,
    )
    band_keys = jnp.concatenate([prior_keys, keys_reduced_precision], axis=0)
    band_values = jnp.concatenate([prior_values, value_row_tensor], axis=0)
    padded_docs = jnp.concatenate(
        [
            jnp.full((WINDOW_LENGTH,), -1, jnp.int32),
            doc_ids[0],
            jnp.full((WINDOW_LENGTH,), -2, jnp.int32),
        ],
        axis=0,
    )
    band_docs = lax.dynamic_slice_in_dim(padded_docs, first_row, row_overall_count + WINDOW_LENGTH)
    block_rows = math.gcd(row_overall_count, 64)

    def one_block(block_index, carried):
        query_total, key_full_gathered, value_total = carried
        offset = (block_index * block_rows).astype(jnp.int32)
        query_part, key_part, value_part = band_block(
            lax.dynamic_slice_in_dim(query_row_tensor, offset, block_rows),
            lax.dynamic_slice_in_dim(gradient_rows, offset, block_rows),
            lax.dynamic_slice_in_dim(band_keys, offset, block_rows + WINDOW_LENGTH),
            lax.dynamic_slice_in_dim(band_values, offset, block_rows + WINDOW_LENGTH),
            lax.dynamic_slice_in_dim(band_docs, offset + WINDOW_LENGTH, block_rows),
            lax.dynamic_slice_in_dim(band_docs, offset, block_rows + WINDOW_LENGTH),
        )
        query_total = lax.dynamic_update_slice_in_dim(query_total, query_part, offset, 0)
        key_full_gathered = lax.dynamic_update_slice_in_dim(
            key_full_gathered,
            lax.dynamic_slice_in_dim(key_full_gathered, offset, block_rows + WINDOW_LENGTH)
            + key_part,
            offset,
            0,
        )
        value_total = lax.dynamic_update_slice_in_dim(
            value_total,
            lax.dynamic_slice_in_dim(value_total, offset, block_rows + WINDOW_LENGTH) + value_part,
            offset,
            0,
        )
        return (query_total, key_full_gathered, value_total)

    start_totals = (
        jnp.zeros((row_overall_count, QUERY_HEAD_COUNT * HEAD_SIZE), jnp.float32),
        jnp.zeros((row_overall_count + WINDOW_LENGTH, KEY_FEATURES), jnp.float32),
        jnp.zeros((row_overall_count + WINDOW_LENGTH, KEY_FEATURES), jnp.float32),
    )
    query_total, key_full_gathered, value_total = lax.fori_loop(
        0, row_overall_count // block_rows, one_block, start_totals
    )
    key_local_shard = key_full_gathered[WINDOW_LENGTH:]
    value_own = value_total[WINDOW_LENGTH:]
    incoming_keys, incoming_values = passed_along(
        (key_full_gathered[:WINDOW_LENGTH], value_total[:WINDOW_LENGTH]), "ctx", -1
    )
    key_local_shard = key_local_shard.at[row_overall_count - WINDOW_LENGTH :].add(incoming_keys)
    value_own = value_own.at[row_overall_count - WINDOW_LENGTH :].add(incoming_values)
    key_linear_gradient = (
        invert_rotary(
            key_local_shard.reshape(row_overall_count, KEY_VALUE_HEADS, HEAD_SIZE),
            cosine_table,
            sine_table,
        )
        .reshape(row_overall_count, KEY_FEATURES)
        .astype(jnp.bfloat16)
    )
    input_grad = lax.dot_general(
        key_linear_gradient,
        full_weight,
        (((1,), (1,)), ((), ())),
        preferred_element_type=jnp.float32,
    ).astype(jnp.bfloat16)
    weight_term = lax.dot_general(
        inputs, key_linear_gradient, (((0,), (0,)), ((), ())), preferred_element_type=jnp.float32
    )
    ctx_summed = lax.psum_scatter(weight_term, "ctx", scatter_dimension=1, tiled=True)
    weight_grad = lax.psum_scatter(ctx_summed, "dp", scatter_dimension=0, tiled=True)
    return (
        query_total.astype(jnp.bfloat16)[None],
        value_own.astype(jnp.bfloat16)[None],
        input_grad[None],
        weight_grad,
    )


def solution(mesh):
    in_specs = (
        P("dp", "ctx", None),
        P("dp", "ctx", None),
        P("dp", "ctx", None),
        P("dp", "ctx"),
        P("dp", "ctx", None),
        P("dp", None),
    )
    out_specs = (P("dp", "ctx", None), P("dp", "ctx", None), P("dp", "ctx", None), P("dp", "ctx"))
    return jax.shard_map(
        per_device, mesh=mesh, in_specs=in_specs, out_specs=out_specs, check_vma=False
    )
```

profile of v0, /device:TPU:8, one launch (start us, length us, event | category | flops | bytes accessed | tf_op | source)
XLA Modules:
  0.0 667.4 jit_solution(4894691800407184521)
XLA Ops:
  7.2 59.7 %all_gather.6 = bf16[180,256]{0,1:T(8,128)(2,1)S(1)} all-gather(bf16[180,8]{0,1:T(8,128)(2,1)} %param.15), channel_id=1, replica_groups=mesh['dp'=16,'ctx'=32] {'ctx'}, dimensions={1}, use_global_device_ids=true | all-gather | bytes 95040 | tf_op jit(solution)/shard_map/all_gather | solution.py:125
  67.8 1.0 copy.55
  68.9 2.3 collective-permute-start.1
  71.4 1.4 fusion.26
  72.8 73.7 %all-gather.3.cloned.1.call-done = bf16[16,180,256]{2,1,0:T(8,128)(2,1)} async-done(((bf16[1,180,256]{2,1,0:T(8,128)(2,1)}), bf16[16,180,256]{2,1,0:T(8,128)(2,1)}) %all-gather.3.cloned.1.call-update) | async-done | bytes 1474576 | tf_op jit(solution)/shard_map/all_gather | solution.py:126
  146.5 2.3 reshape.265
  148.8 1.7 copy.54
  150.5 2.0 fusion.21
  152.6 1.3 collective-permute-start
  156.3 1.0 broadcast_in_dim.79.clone
  157.3 57.0 %while.21 = (s32[]{:T(128)}, bf16[192,2048]{1,0:T(8,128)(2,1)}, f32[320,256]{0,1:T(8,128)S(1)}, f32[320,256]{1,0:T(8,128)}, bf16[320,256]{0,1:T(8,128)(2,1)}, /*...) while((s32[]{:T(128)}, bf16[192,2048]{1,0:T(8,128)(2,1)}, ...), condition=%wide.region_4.5_spmd, body=%wide.region_0.4_spmd.sunk | while | flops 306796800 | bytes 18583368 | solution.py:197
  159.5 0.9 constant_dynamic-slice_fusion.12
  160.6 1.1 constant_dynamic-slice_fusion.10
  161.6 1.1 constant_dynamic-slice_fusion.11
  163.3 2.9 fusion.77
  166.1 1.9 fusion.78
  168.1 1.2 fusion.79
  169.9 2.2 fusion.80
  173.4 1.5 dynamic_update_slice.37
  178.5 0.9 constant_dynamic-slice_fusion.12
  179.6 1.1 constant_dynamic-slice_fusion.10
  180.7 1.1 constant_dynamic-slice_fusion.11
  182.3 2.9 fusion.77
  185.2 1.9 fusion.78
  187.1 1.2 fusion.79
  188.9 2.2 fusion.80
  192.4 1.8 dynamic_update_slice.37
  199.0 1.1 constant_dynamic-slice_fusion.10
  200.1 1.1 constant_dynamic-slice_fusion.11
  201.7 2.9 fusion.77
  204.6 1.9 fusion.78
  206.5 1.2 fusion.79
  208.3 2.2 fusion.80
  211.8 1.1 dynamic_update_slice.37
  214.3 1.3 collective-permute-start.3
  215.6 4.0 collective-permute-done.3
  219.8 1.3 scatter-add.9
  221.9 2.3 convolution_bitcast_fusion.2
  225.2 1.3 collective-permute-start.2
  226.5 1.3 dynamic-slice.22
  228.5 1.3 dynamic-slice.16
  230.4 0.9 slice.82
  233.1 364.7 %all-reduce.5.cloned.1.call-done = f32[2880,256]{1,0:T(8,128)} async-done(((f32[2880,256]{1,0:T(8,128)}), f32[2880,256]{1,0:T(8,128)}) %all-reduce.5.cloned.1.call-update) | async-done | bytes 2949136
  597.8 2.9 constant_dynamic-slice_fusion.6
  600.8 49.3 %fusion = f32[192,8]{1,0:T(8,128)S(1)} fusion(f32[2880,8]{1,0:T(8,128)} %constant_dynamic-slice_fusion.6), kind=kCustom, calls=%all-reduce-scatter | all-reduce-scatter fusion | flops 24577 | bytes 100352
  650.1 3.5 collective-permute-start.4
  653.7 1.6 fusion.20
  655.3 4.2 collective-permute-done.4
  (99 shorter events, 27.7 us)
Async XLA Ops:
  7.2 143.3 %copy-start = (bf16[1,192,2880]{2,1,0:T(8,128)(2,1)S(1)}, bf16[1,192,2880]{2,1,0:T(8,128)(2,1)}, u32[]{:S(2)}) copy-start(bf16[1,192,2880]{2,1,0:T(8,128)(2,1)} %param.12) | copy-start | bytes 3317764
  7.2 139.3 %all-gather.3.cloned.1.call-start = ((), (), s32[]{:S(2)}) async-start(), calls=%async_computation | async-start | bytes 1601536 | tf_op jit(solution)/shard_map/all_gather | solution.py:126
  67.7 530.1 %all-reduce.5.cloned.1.call-start = ((), (), s32[]{:S(2)}) async-start(), calls=%async_computation.1 | async-start | bytes 5898240
  68.9 3.9 collective-permute-start.1
  71.4 81.1 %copy-start.4 = (f32[192,32]{0,1:T(8,128)}, f32[192,32]{0,1:T(8,128)S(1)}, u32[]{:S(2)}) copy-start(f32[192,32]{0,1:T(8,128)S(1)} %get-tuple-element.297) | copy-start | bytes 73732
  71.4 81.1 %copy-start.5 = (f32[192,32]{0,1:T(8,128)}, f32[192,32]{0,1:T(8,128)S(1)}, u32[]{:S(2)}) copy-start(f32[192,32]{0,1:T(8,128)S(1)} %get-tuple-element.298) | copy-start | bytes 73732
  148.8 3.7 copy-start.1
  152.6 2.2 collective-permute-start
  166.1 3.2 copy-start.3
  185.2 3.2 copy-start.3
  204.5 3.2 copy-start.3
  214.3 5.4 collective-permute-start.3
  225.2 6.9 %collective-permute-start.2 = (f32[128,256]{1,0:T(8,128)S(1)}, f32[128,256]{1,0:T(8,128)S(1)}, u32[]{:S(2)}, u32[]{:S(2)}) collective-permute-start(f32[128,256]{1,0:T(8,128)S(1)} %slice.84), channel_id=1, source_target_pairs={{1,0},{2,1},{3,2},{4,3},{5,4},{6,5},{7,6},{8,7},{9,8},{10,9},{11,1... | collective-permute-start | bytes 393224 | tf_op jit(solution)/shard_map/ppermute | solution.py:22
  233.1 417.0 %copy-start.6 = (bf16[192,256]{1,0:T(8,128)(2,1)}, bf16[192,256]{1,0:T(8,128)(2,1)S(1)}, u32[]{:S(2)}) copy-start(bf16[192,256]{1,0:T(8,128)(2,1)S(1)} %add_dynamic-update-slice_fusion) | copy-start | bytes 294916
  233.1 420.6 %copy-start.2 = (bf16[2880,256]{1,0:T(8,128)(2,1)S(1)}, bf16[2880,256]{1,0:T(8,128)(2,1)}, u32[]{:S(2)}) copy-start(bf16[2880,256]{1,0:T(8,128)(2,1)} %copy-done.1) | copy-start | bytes 4423684
  650.1 9.4 %collective-permute-start.4 = (f32[180,8]{1,0:T(8,128)S(1)}, f32[180,8]{1,0:T(8,128)S(1)}, u32[]{:S(2)}, u32[]{:S(2)}) collective-permute-start(f32[180,8]{1,0:T(8,128)S(1)} %slice.97), channel_id=1, source_target_pairs={{0,32},{32,64},{64,96},{96,128},{128,160},{160,192},{192,224},{224... | collective-permute-start | bytes 17288
Sparse Core Ops, SparseCore 0:
  67.8 78.6 all-gather.2
  224.4 373.3 all-reduce.4
where the time goes:
time: 669 us; the launch traced here: 667 us
  waiting for transfers between devices  448 us (67%)
  blocking collectives  109 us (16%)
  local copies, waits for them, and re-layouts  42.8 us (6%)
  matrix products  28.7 us (4%)
  between operations  15.7 us (2%)
  other arithmetic  12.8 us (2%)
  starting transfers between devices  9.73 us (1%)
    unnamed x4, waiting for transfers between devices  369 us
    all_gather x1, waiting for transfers between devices, per_device(): full_weight = lax.all_gather(columns, 'dp', axis=0, tiled=True)  73.7 us
    all_gather x1, blocking collectives, per_device(): columns = lax.all_gather(key_weight, 'ctx', axis=1, tiled=True)  59.7 us
    unnamed x1, blocking collectives  49.3 us
  transfers between devices with their start and end apart: 7, of which 6 were waited for; matrix products, arithmetic and copies ran while one was open for 1% of the time, Pallas kernels for 0%

commit v1 on v0

v1 whole, which is shorter than its diff:
```python
import jax
import jax.numpy as jnp
from jax import lax
from jax.experimental import pallas as pl
from jax.experimental.pallas import tpu as pltpu
from jax.sharding import Mesh
from jax.sharding import PartitionSpec as P

QUERY_HEADS = 32
KV_HEADS = 4
HEAD = 64
WINDOW = 128
KEYF = 256
GROUP = QUERY_HEADS // KV_HEADS
ROWS = 64
rope_base = 150000.0
masked_score = -1e30
bf16 = jnp.bfloat16
f32 = jnp.float32

DP = ("zl", "y")
CTX = ("zh", "x", "core")
Z = ("zl", "zh")


def nt(a, b):
    return lax.dot_general(a, b, (((1,), (1,)), ((), ())), preferred_element_type=f32)


def nn(a, b):
    return lax.dot_general(a, b, (((1,), (0,)), ((), ())), preferred_element_type=f32)


def tn(a, b):
    return lax.dot_general(a, b, (((0,), (0,)), ((), ())), preferred_element_type=f32)


def swap_halves(x):
    lane = lax.broadcasted_iota(jnp.int32, x.shape, 1)
    width = x.shape[1]
    return jnp.where(lane % HEAD < HEAD // 2, pltpu.roll(x, width - HEAD // 2, 1), pltpu.roll(x, HEAD // 2, 1))


def project_kernel(tokens_ref, weight_ref, cos_ref, sin_ref, keys_ref):
    linear = nt(tokens_ref[...], weight_ref[...])
    keys_ref[...] = (linear * cos_ref[...] + swap_halves(linear) * sin_ref[...]).astype(bf16)


def doubled(tile, parity):
    wide = tile.astype(f32)
    lane = lax.broadcasted_iota(jnp.int32, wide.shape, 1)
    return jnp.where(lane // HEAD == parity, wide, pltpu.roll(wide, HEAD, 1))


def attention_kernel(
    q_ref, g_ref, k_ref, v_ref, hk_ref, hv_ref, qd_ref, kd_ref, dq_ref, dk_ref, dv_ref,
    bias_ref, kk_ref, vv_ref, dka_ref, dva_ref,
):
    step = pl.program_id(0)
    parity = step % 2
    rows = q_ref.shape[0]
    span = ROWS + WINDOW
    lanes = GROUP * ROWS
    blocks = rows // ROWS

    @pl.when(step == 0)
    def _():
        key_at = lax.broadcasted_iota(jnp.int32, (span, lanes), 0)
        query_at = lax.broadcasted_iota(jnp.int32, (span, lanes), 1) % ROWS
        distance = query_at + WINDOW - key_at
        near = (distance >= 0) & (distance <= WINDOW)
        for b in range(blocks):
            same = kd_ref[b * ROWS : b * ROWS + span, :] == qd_ref[b]
            bias_ref[b] = jnp.where(near & same, 0.0, masked_score)

    kk_ref[:WINDOW, :] = (doubled(hk_ref[...], parity) * 0.125).astype(bf16)
    kk_ref[WINDOW:, :] = (doubled(k_ref[...], parity) * 0.125).astype(bf16)
    vv_ref[:WINDOW, :] = doubled(hv_ref[...], parity).astype(bf16)
    vv_ref[WINDOW:, :] = doubled(v_ref[...], parity).astype(bf16)
    dka_ref[...] = jnp.zeros_like(dka_ref)
    dva_ref[...] = jnp.zeros_like(dva_ref)
    lane = lax.broadcasted_iota(jnp.int32, (ROWS, 2 * HEAD), 1)
    low = jnp.where(lane < HEAD, 1.0, 0.0).astype(bf16)
    high = jnp.where(lane < HEAD, 0.0, 1.0).astype(bf16)

    def stacked(ref, b):
        parts = []
        for p in range(GROUP // 2):
            pair = ref[b * ROWS : (b + 1) * ROWS, p * 2 * HEAD : (p + 1) * 2 * HEAD]
            parts += [pair * low, pair * high]
        return jnp.concatenate(parts, axis=0)

    for b in range(blocks):
        band = slice(b * ROWS, b * ROWS + span)
        keys = kk_ref[band, :]
        values = vv_ref[band, :]
        qs = stacked(q_ref, b)
        gs = stacked(g_ref, b)
        scores = nt(keys, qs) + bias_ref[b]
        weights = jnp.exp(scores - jnp.max(scores, axis=0, keepdims=True))
        probs = weights * (1.0 / jnp.sum(weights, axis=0, keepdims=True))
        probs_low = probs.astype(bf16)
        prob_grad = nt(values, gs)
        delta = jnp.sum(probs_low.astype(f32) * prob_grad, axis=0, keepdims=True)
        score_low = (probs * (prob_grad - delta)).astype(bf16)
        dva_ref[band, :] += nn(probs_low, gs)
        dka_ref[band, :] += nn(score_low, qs)
        dq = tn(score_low, keys)
        for p in range(GROUP // 2):
            top = dq[2 * p * ROWS : (2 * p + 1) * ROWS]
            bottom = dq[(2 * p + 1) * ROWS : (2 * p + 2) * ROWS]
            dq_ref[b * ROWS : (b + 1) * ROWS, p * 2 * HEAD : (p + 1) * 2 * HEAD] = jnp.where(
                lane < HEAD, top, bottom
            ).astype(bf16)

    wide = lax.broadcasted_iota(jnp.int32, dka_ref.shape, 1)
    mine = wide // HEAD == parity
    dk = dka_ref[...] * 0.125
    dv = dva_ref[...]
    dk_ref[...] = jnp.where(mine, dk + pltpu.roll(dk, HEAD, 1), dk_ref[...])
    dv_ref[...] = jnp.where(mine, dv + pltpu.roll(dv, HEAD, 1), dv_ref[...])


def tail_kernel(
    dk_ref, dv_ref, inc_ref, cos_ref, sin_ref, tokens_ref, weight_ref, order_ref,
    vg_ref, ig_ref, own_ref, send_ref,
):
    rows = tokens_ref.shape[0]
    edge = rows - WINDOW
    vg_ref[:edge, :] = dv_ref[WINDOW : WINDOW + edge, :].astype(bf16)
    vg_ref[edge:, :] = (dv_ref[WINDOW + edge :, :] + inc_ref[:, KEYF:]).astype(bf16)
    dk = jnp.concatenate(
        [dk_ref[WINDOW : WINDOW + edge, :], dk_ref[WINDOW + edge :, :] + inc_ref[:, :KEYF]], axis=0
    )
    lin = (dk * cos_ref[...] - swap_halves(dk) * sin_ref[...]).astype(bf16)
    ordered = nt(order_ref[...], lin).astype(bf16)
    half = KEYF // 2
    own_ref[...] = nn(ordered[:half], tokens_ref[...])
    send_ref[...] = nn(ordered[half:], tokens_ref[...]).astype(bf16)
    ig_ref[...] = nn(lin, weight_ref[...]).astype(bf16)


def spread(x, axes):
    peers = lax.axis_size(axes)
    return lax.all_to_all(jnp.broadcast_to(x[None], (peers,) + x.shape), axes, 0, 0, tiled=True)


def exchanged(x, axis):
    return lax.ppermute(x, axis, [(0, 1), (1, 0)])


def gathered_weight(block):
    width = block.shape[0]
    sub = block.shape[1]
    zl, y, zh, x = (lax.axis_size(a) for a in ("zl", "y", "zh", "x"))
    along_z = spread(block.T, Z)
    along_y = spread(along_z, "y")
    rows = along_y.reshape(y, zl, zh, sub, width).transpose(2, 3, 1, 0, 4).reshape(zh, sub, zl * y * width)
    along_x = lax.all_gather(rows, "x", axis=0)
    other = exchanged(along_x, "core")
    first = lax.axis_index("core") == 0
    pair = jnp.stack([jnp.where(first, along_x, other), jnp.where(first, other, along_x)], axis=2)
    return pair.transpose(1, 0, 2, 3, 4).reshape(zh * x * 2 * sub, zl * y * width)


def scattered_gradient(own, send, width, sub):
    zl, y, zh, x = (lax.axis_size(a) for a in ("zl", "y", "zh", "x"))
    both = (own + exchanged(send, "core").astype(f32)).astype(bf16)
    both = both.reshape(x, zh, sub, zl * y * width)
    over_x = jnp.sum(lax.all_to_all(both, "x", 0, 0, tiled=True).astype(f32), axis=0).astype(bf16)
    over_x = over_x.reshape(zh, sub, zl, y, width).transpose(3, 2, 0, 1, 4).reshape(y, zl * zh, sub, width)
    over_y = jnp.sum(lax.all_to_all(over_x, "y", 0, 0, tiled=True).astype(f32), axis=0).astype(bf16)
    return jnp.sum(lax.all_to_all(over_y, Z, 0, 0, tiled=True).astype(f32), axis=0)


def per_device(tokens_in, queries, values_in, key_weight, out_grad, doc_ids):
    rows = tokens_in.shape[1]
    dim = tokens_in.shape[2]
    width, sub = key_weight.shape
    tokens, q, g, v = tokens_in[0], queries[0], out_grad[0], values_in[0]
    blocks = rows // ROWS
    peers = lax.axis_size(CTX)
    position = lax.axis_index(CTX)
    first_row = position * rows

    exponent = jnp.arange(HEAD // 2, dtype=f32) * (-2.0 / HEAD)
    inverse_freq = jnp.power(f32(rope_base), exponent)
    angles = (first_row + jnp.arange(rows, dtype=jnp.int32)).astype(f32)[:, None] * inverse_freq[None, :]
    cosine, sine = jnp.cos(angles), jnp.sin(angles)
    cos_table = jnp.tile(cosine, (1, 2 * KV_HEADS))
    sin_table = jnp.tile(jnp.concatenate([-sine, sine], axis=1), (1, KV_HEADS))

    padded_docs = jnp.concatenate([jnp.full((WINDOW,), -1, jnp.int32), doc_ids[0]])
    band_docs = lax.dynamic_slice_in_dim(padded_docs, first_row, rows + WINDOW)
    query_docs = jnp.tile(band_docs[WINDOW:].reshape(blocks, 1, ROWS), (1, 1, GROUP))
    key_docs = band_docs[:, None]

    core = lax.axis_index("core")
    zh, x = lax.axis_size("zh"), lax.axis_size("x")
    dest = jnp.arange(KEYF, dtype=jnp.int32)
    rel, dest_x, dest_zh, dest_j = dest // 128, dest // 32 % 4, dest // 8 % 4, dest % 8
    source = dest_zh * 64 + dest_x * 16 + (rel ^ core) * 8 + dest_j
    order = (source[:, None] == jnp.arange(KEYF, dtype=jnp.int32)[None, :]).astype(bf16)

    weight = gathered_weight(key_weight)

    params = pltpu.CompilerParams(vmem_limit_bytes=40 << 20)
    keys = pl.pallas_call(
        project_kernel,
        out_shape=jax.ShapeDtypeStruct((rows, KEYF), bf16),
        compiler_params=params,
        name="project",
    )(tokens, weight, cos_table, sin_table)

    along = [(i, i + 1) for i in range(peers - 1)]
    back = [(i + 1, i) for i in range(peers - 1)]
    halo = lax.ppermute(jnp.concatenate([keys[rows - WINDOW :], v[rows - WINDOW :]], axis=1), CTX, along)

    span = ROWS + WINDOW
    dq, dk, dv = pl.pallas_call(
        attention_kernel,
        grid=(KV_HEADS,),
        in_specs=[
            pl.BlockSpec((rows, GROUP * HEAD), lambda k: (0, k)),
            pl.BlockSpec((rows, GROUP * HEAD), lambda k: (0, k)),
            pl.BlockSpec((rows, 2 * HEAD), lambda k: (0, k // 2)),
            pl.BlockSpec((rows, 2 * HEAD), lambda k: (0, k // 2)),
            pl.BlockSpec((WINDOW, 2 * HEAD), lambda k: (0, k // 2)),
            pl.BlockSpec((WINDOW, 2 * HEAD), lambda k: (0, 2 + k // 2)),
            pl.BlockSpec((blocks, 1, GROUP * ROWS), lambda k: (0, 0, 0)),
            pl.BlockSpec((rows + WINDOW, 1), lambda k: (0, 0)),
        ],
        out_specs=[
            pl.BlockSpec((rows, GROUP * HEAD), lambda k: (0, k)),
            pl.BlockSpec((rows + WINDOW, 2 * HEAD), lambda k: (0, k // 2)),
            pl.BlockSpec((rows + WINDOW, 2 * HEAD), lambda k: (0, k // 2)),
        ],
        out_shape=[
            jax.ShapeDtypeStruct((rows, QUERY_HEADS * HEAD), bf16),
            jax.ShapeDtypeStruct((rows + WINDOW, KEYF), f32),
            jax.ShapeDtypeStruct((rows + WINDOW, KEYF), f32),
        ],
        scratch_shapes=[
            pltpu.VMEM((blocks, span, GROUP * ROWS), f32),
            pltpu.VMEM((rows + WINDOW, 2 * HEAD), bf16),
            pltpu.VMEM((rows + WINDOW, 2 * HEAD), bf16),
            pltpu.VMEM((rows + WINDOW, 2 * HEAD), f32),
            pltpu.VMEM((rows + WINDOW, 2 * HEAD), f32),
        ],
        compiler_params=params,
        name="band_attention",
    )(q, g, keys, v, halo, halo, query_docs, key_docs)

    incoming = lax.ppermute(jnp.concatenate([dk[:WINDOW], dv[:WINDOW]], axis=1), CTX, back)

    value_grad, input_grad, own, send = pl.pallas_call(
        tail_kernel,
        out_shape=[
            jax.ShapeDtypeStruct((rows, KEYF), bf16),
            jax.ShapeDtypeStruct((rows, dim), bf16),
            jax.ShapeDtypeStruct((KEYF // 2, dim), f32),
            jax.ShapeDtypeStruct((KEYF // 2, dim), bf16),
        ],
        compiler_params=params,
        name="tail",
    )(dk, dv, incoming, cos_table, sin_table, tokens, weight, order)

    weight_grad = scattered_gradient(own, send, width, sub).T
    return dq[None], value_grad[None], input_grad[None], weight_grad


def solution(mesh):
    fine = Mesh(mesh.devices.reshape(4, 4, 4, 4, 2), ("zl", "y", "zh", "x", "core"))
    rows = P(DP, CTX, None)
    square = P(DP, CTX)
    return jax.shard_map(
        per_device,
        mesh=fine,
        in_specs=(rows, rows, rows, square, rows, P(DP, None)),
        out_specs=(rows, rows, rows, square),
        check_vma=False,
    )
```

time: 669 us -> 159 us (0.24)
  the two profiles are of different devices: /device:TPU:8 before, /device:TPU:32 now
where the time goes in v1:
time: 159 us; the launch traced here: 158 us
  blocking collectives  102 us (64%)
  starting transfers between devices  17 us (11%)
  waiting for transfers between devices  14 us (9%)
  Pallas kernels  11.1 us (7%)
  local copies, waits for them, and re-layouts  11 us (7%)
  other arithmetic  2.25 us (1%)
    all_to_all x1, blocking collectives, scattered_gradient(): lax.all_to_all(both, 'x', 0, 0, tiled=True).astype(f32)  31.4 us
    all_to_all x1, blocking collectives, spread(): lax.all_to_all(jnp.broadcast_to(x[None], (peers,) + x.shape), axes, 0, 0,...  27.2 us
    all_to_all x1, blocking collectives, scattered_gradient(): lax.all_to_all(over_y, Z, 0, 0, tiled=True).astype(f32)  20.2 us
    all_gather x1, blocking collectives, gathered_weight(): along_x = lax.all_gather(rows, 'x', axis=0)  14.3 us
    ppermute x2, starting transfers between devices, exchanged(): return lax.ppermute(x, axis, [(0, 1), (1, 0)])  9.19 us
    all_to_all x1, blocking collectives, scattered_gradient(): lax.all_to_all(over_x, 'y', 0, 0, tiled=True).astype(f32)  9.07 us
    pallas_call x1, Pallas kernels, per_device(): pl.pallas_call(attention_kernel, grid=(KV_HEADS,), in_specs=[pl.BlockSpec...  8.1 us
    all_to_all x1, waiting for transfers between devices, spread(): lax.all_to_all(jnp.broadcast_to(x[None], (peers,) + x.shape), axes, 0, 0,...  6.68 us
  transfers between devices with their start and end apart: 5, of which 5 were waited for; matrix products, arithmetic and copies ran while one was open for 1% of the time, Pallas kernels for 0%

profile of v1, /device:TPU:32, one launch (start us, length us, event | category | flops | bytes accessed | tf_op | source)
XLA Modules:
  0.0 158.3 jit_solution(3368810424762971069)
XLA Ops:
  0.6 0.7 broadcast_in_dim.12
  1.3 27.2 %all_to_all.25 = bf16[16,8,180]{2,1,0:T(8,128)(2,1)S(1)} all-to-all(bf16[16,8,180]{2,1,0:T(8,128)(2,1)S(1)} %broadcast_in_dim.12), channel_id=1, replica_groups=mesh['zl'=4,'y'=4,'zh'=4,'x'=4,'core'=2] {'zl','zh'}, dimensions={0} | all-to-all | bytes 92160 | tf_op jit(solution)/shard_map/all_to_all | solution.py:145
  28.5 0.7 broadcast_in_dim.13
  29.2 4.5 %all-to-all-start.1 = ((bf16[4,16,8,180]{3,2,1,0:T(8,128)(2,1)}), bf16[4,16,8,180]{3,2,1,0:T(8,128)(2,1)S(1)}, u32[]{:S(2)}, u32[]{:S(2)}) async-start(bf16[4,16,8,180]{3,2,1,0:T(8,128)(2,1)} %broadcast_in_dim.13), calls=%async_computation.1 | async-start | bytes 524288 | tf_op jit(solution)/shard_map/all_to_all | solution.py:145
  33.7 6.7 %all-to-all-done.1 = bf16[4,16,8,180]{3,2,1,0:T(8,128)(2,1)S(1)} async-done(((bf16[4,16,8,180]{3,2,1,0:T(8,128)(2,1)}), bf16[4,16,8,180]{3,2,1,0:T(8,128)(2,1)S(1)}, u32[]{:S(2)}, u32[]{:S(2)}) %all-to-all-start.1) | async-done | bytes 184352 | tf_op jit(solution)/shard_map/all_to_all | solution.py:145
  40.3 0.2 copy.35
  40.5 0.0 copy-start.6
  40.6 0.4 all_gather_reshape.3
  40.9 14.3 %all_gather.3 = bf16[4,4,8,2880]{3,2,1,0:T(8,128)(2,1)S(1)} all-gather(bf16[1,4,8,2880]{3,2,1,0:T(8,128)(2,1)S(1)} %all_gather_reshape.3), channel_id=1, replica_groups=mesh['zl'=4,'y'=4,'zh'=4,'x'=4,'core'=2] {'x'}, dimensions={0}, use_global_device_ids=true | all-gather | bytes 921600 | tf_op jit(solution)/shard_map/all_gather | solution.py:159
  55.2 1.9 %collective-permute-start = (bf16[4,4,8,2880]{3,2,1,0:T(8,128)(2,1)S(1)}, bf16[4,4,8,2880]{3,2,1,0:T(8,128)(2,1)S(1)}, u32[]{:S(2)}, u32[]{:S(2)}) collective-permute-start(bf16[4,4,8,2880]{3,2,1,0:T(8,128)(2,1)S(1)} %all_gather.3), channel_id=1, source_target_pairs={{0,1},{1,0},{2,3},{3,2},{4,5},{5,4},{6,7},{7,6},{8,9},{9,8},{10,11... | collective-permute-start | bytes 2211848 | tf_op jit(solution)/shard_map/ppermute | solution.py:149
  57.1 0.2 fusion.1
  57.4 0.1 copy.38.sin_ref
  57.5 0.1 copy.37.cos_ref
  57.7 1.6 %collective-permute-done = bf16[4,4,8,2880]{3,2,1,0:T(8,128)(2,1)S(1)} collective-permute-done((bf16[4,4,8,2880]{3,2,1,0:T(8,128)(2,1)S(1)}, bf16[4,4,8,2880]{3,2,1,0:T(8,128)(2,1)S(1)}, u32[]{:S(2)}, u32[]{:S(2)}) %collective-permute-start) | collective-permute-done | bytes 737312 | tf_op jit(solution)/shard_map/ppermute | solution.py:149
  59.3 0.1 select_bitcast_fusion.1
  59.5 0.2 maximum_bitcast_fusion
  59.6 0.0 copy-start
  59.6 0.1 copy.36
  59.8 1.1 copy-done
  60.9 0.8 project.1.k_ref
  61.7 0.7 pad_maximum_fusion.1
  62.3 2.0 %collective-permute-start.1 = (bf16[128,512]{1,0:T(8,128)(2,1)}, bf16[128,512]{1,0:T(8,128)(2,1)S(1)}, u32[]{:S(2)}, u32[]{:S(2)}) collective-permute-start(bf16[128,512]{1,0:T(8,128)(2,1)} %pad_maximum_fusion.1), channel_id=1, source_target_pairs={{0,1},{1,2},{2,3},{3,4},{4,5},{5,6},{6,7},{7,8},{8,9},{9,10},{10,1... | collective-permute-start | bytes 393224 | tf_op jit(solution)/shard_map/ppermute | solution.py:217
  64.4 0.1 pad_dynamic-slice_fusion
  64.5 0.1 broadcast_in_dim.35.kd_ref
  64.6 0.1 tile.32
  64.7 0.1 tile.34.qd_ref
  64.8 0.8 collective-permute-done.1.hk_ref.hv_ref
  65.5 1.1 copy-done.3
  66.7 1.1 copy-done.4
  67.8 8.1 %band_attention.1 = (bf16[192,2048]{1,0:T(8,128)(2,1)}, f32[320,256]{1,0:T(8,128)S(1)}, f32[320,256]{1,0:T(8,128)S(1)}) custom-call(bf16[192,2048]{1,0:T(8,128)(2,1)S(1)} %bitcast.31, bf16[192,2048]{1,0:T(8,128)(2,1)S(1)} %bitcast.32, bf16[192,256]{1,0:T(8,128)(2,1)S(1)} %project.1.k_ref, bf16[192,256]{1,0:T(8,128)(2,1)S(1)} %bitcast.33, ...), custom_call_target="tpu_custom_call" | custom-call | tf_op jit(solution)/shard_map/band_attention/pallas_call | solution.py:220
  76.0 1.3 collective-permute-start.2
  77.3 0.1 fusion.order_ref
  77.4 3.1 %collective-permute-done.2.inc_ref = f32[128,512]{1,0:T(8,128)S(1)} collective-permute-done((f32[128,512]{1,0:T(8,128)S(1)}, f32[128,512]{1,0:T(8,128)S(1)}, u32[]{:S(2)}, u32[]{:S(2)}) %collective-permute-start.2) | collective-permute-done | bytes 262176 | tf_op jit(solution)/shard_map/ppermute | solution.py:254
  80.5 2.2 %tail.1 = (bf16[192,256]{1,0:T(8,128)(2,1)}, bf16[192,2880]{1,0:T(8,128)(2,1)}, f32[128,2880]{1,0:T(8,128)S(1)}, bf16[128,2880]{1,0:T(8,128)(2,1)S(1)}) custom-call(f32[320,256]{1,0:T(8,128)S(1)} %get-tuple-element.12.dk_ref, f32[320,256]{1,0:T(8,128)S(1)} %get-tuple-element.13.dv_ref, f32[128,512]{1,0:T(8,128)S(1)} %collective-permute-done.2.inc_ref, ...), custom_call_target="tpu_custom_call" | custom-call | tf_op jit(solution)/shard_map/tail/pallas_call | solution.py:256
  82.7 1.1 copy-done.1
  83.8 0.9 copy-done.5
  84.7 1.6 %copy.42 = bf16[128,2880]{0,1:T(8,128)(2,1)S(1)} copy(bf16[128,2880]{1,0:T(8,128)(2,1)} %copy-done.5) | data formatting | bytes 1474560 | tf_op jit(solution)/shard_map/tail/pallas_call | solution.py:256
  86.3 7.3 %collective-permute-start.3 = (bf16[128,2880]{0,1:T(8,128)(2,1)S(1)}, bf16[128,2880]{0,1:T(8,128)(2,1)S(1)}, u32[]{:S(2)}, u32[]{:S(2)}) collective-permute-start(bf16[128,2880]{0,1:T(8,128)(2,1)S(1)} %copy.42), channel_id=1, source_target_pairs={{0,1},{1,0},{2,3},{3,2},{4,5},{5,4},{6,7},{7,6},{8,9},{9,8},{10,11... | collective-permute-start | bytes 2211848 | tf_op jit(solution)/shard_map/ppermute | solution.py:149
  93.6 1.8 %collective-permute-done.3 = bf16[128,2880]{0,1:T(8,128)(2,1)S(1)} collective-permute-done((bf16[128,2880]{0,1:T(8,128)(2,1)S(1)}, bf16[128,2880]{0,1:T(8,128)(2,1)S(1)}, u32[]{:S(2)}, u32[]{:S(2)}) %collective-permute-start.3) | collective-permute-done | bytes 737312 | tf_op jit(solution)/shard_map/ppermute | solution.py:149
  95.4 0.3 copy.43
  95.8 0.1 add_convert_fusion
  95.9 31.4 %all_to_all.26 = bf16[4,4,8,2880]{3,2,1,0:T(8,128)(2,1)S(1)} all-to-all(bf16[4,4,8,2880]{3,2,1,0:T(8,128)(2,1)S(1)} %bitcast.34), channel_id=1, replica_groups=mesh['zl'=4,'y'=4,'zh'=4,'x'=4,'core'=2] {'x'}, dimensions={0} | all-to-all | bytes 1474560 | tf_op jit(solution)/shard_map/all_to_all | solution.py:170
  127.3 0.1 reduce_sum.33
  127.5 0.8 reshape.150
  128.3 0.1 copy.44
  128.3 9.1 %all_to_all.27 = bf16[4,16,8,180]{3,2,1,0:T(8,128)(2,1)S(1)} all-to-all(bf16[4,16,8,180]{3,2,1,0:T(8,128)(2,1)S(1)} %bitcast.39), channel_id=1, replica_groups=mesh['zl'=4,'y'=4,'zh'=4,'x'=4,'core'=2] {'y'}, dimensions={0} | all-to-all | bytes 368640 | tf_op jit(solution)/shard_map/all_to_all | solution.py:172
  137.5 20.2 %all_to_all.28 = bf16[16,8,180]{2,1,0:T(8,128)(2,1)S(1)} all-to-all(bf16[16,8,180]{2,1,0:T(8,128)(2,1)S(1)} %reduce_sum.34), channel_id=1, replica_groups=mesh['zl'=4,'y'=4,'zh'=4,'x'=4,'core'=2] {'zl','zh'}, dimensions={0} | all-to-all | bytes 92160 | tf_op jit(solution)/shard_map/all_to_all | solution.py:173
  157.7 0.6 convert_reduce_fusion
  (23 shorter events, 0.2 us)
Async XLA Ops:
  29.2 11.1 %all-to-all-start.1 = ((bf16[4,16,8,180]{3,2,1,0:T(8,128)(2,1)}), bf16[4,16,8,180]{3,2,1,0:T(8,128)(2,1)S(1)}, u32[]{:S(2)}, u32[]{:S(2)}) async-start(bf16[4,16,8,180]{3,2,1,0:T(8,128)(2,1)} %broadcast_in_dim.13), calls=%async_computation.1 | async-start | bytes 524288 | tf_op jit(solution)/shard_map/all_to_all | solution.py:145
  40.5 17.1 %copy-start.6 = (bf16[1,192,256]{2,1,0:T(8,128)(2,1)S(1)}, bf16[1,192,256]{2,1,0:T(8,128)(2,1)}, u32[]{:S(2)}) copy-start(bf16[1,192,256]{2,1,0:T(8,128)(2,1)} %param.8) | copy-start | bytes 294916
  55.2 4.1 %collective-permute-start = (bf16[4,4,8,2880]{3,2,1,0:T(8,128)(2,1)S(1)}, bf16[4,4,8,2880]{3,2,1,0:T(8,128)(2,1)S(1)}, u32[]{:S(2)}, u32[]{:S(2)}) collective-permute-start(bf16[4,4,8,2880]{3,2,1,0:T(8,128)(2,1)S(1)} %all_gather.3), channel_id=1, source_target_pairs={{0,1},{1,0},{2,3},{3,2},{4,5},{5,4},{6,7},{7,6},{8,9},{9,8},{10,11... | collective-permute-start | bytes 2211848 | tf_op jit(solution)/shard_map/ppermute | solution.py:149
  59.6 1.3 copy-start
  60.9 3.5 %copy-start.7 = (s32[1,6144]{1,0:T(1,128)S(1)}, s32[1,6144]{1,0:T(1,128)}, u32[]{:S(2)}) copy-start(s32[1,6144]{1,0:T(1,128)} %param.11) | copy-start | bytes 73732
  62.3 3.2 %collective-permute-start.1 = (bf16[128,512]{1,0:T(8,128)(2,1)}, bf16[128,512]{1,0:T(8,128)(2,1)S(1)}, u32[]{:S(2)}, u32[]{:S(2)}) collective-permute-start(bf16[128,512]{1,0:T(8,128)(2,1)} %pad_maximum_fusion.1), channel_id=1, source_target_pairs={{0,1},{1,2},{2,3},{3,4},{4,5},{5,6},{6,7},{7,8},{8,9},{9,10},{10,1... | collective-permute-start | bytes 393224 | tf_op jit(solution)/shard_map/ppermute | solution.py:217
  65.5 1.1 copy-start.3
  66.7 1.1 copy-start.4
  76.0 4.5 %collective-permute-start.2 = (f32[128,512]{1,0:T(8,128)S(1)}, f32[128,512]{1,0:T(8,128)S(1)}, u32[]{:S(2)}, u32[]{:S(2)}) collective-permute-start(f32[128,512]{1,0:T(8,128)S(1)} %pad_maximum_fusion), channel_id=1, source_target_pairs={{1,0},{2,1},{3,2},{4,3},{5,4},{6,5},{7,6},{8,7},{9,8},{10,9},{11,1... | collective-permute-start | bytes 786440 | tf_op jit(solution)/shard_map/ppermute | solution.py:254
  82.7 1.1 copy-start.1
  83.8 0.9 copy-start.5
  84.7 11.1 %copy-start.2 = (f32[128,2880]{1,0:T(8,128)S(1)}, f32[128,2880]{1,0:T(8,128)}, u32[]{:S(2)}) copy-start(f32[128,2880]{1,0:T(8,128)} %copy-done.1) | copy-start | bytes 4423684
  86.3 9.1 %collective-permute-start.3 = (bf16[128,2880]{0,1:T(8,128)(2,1)S(1)}, bf16[128,2880]{0,1:T(8,128)(2,1)S(1)}, u32[]{:S(2)}, u32[]{:S(2)}) collective-permute-start(bf16[128,2880]{0,1:T(8,128)(2,1)S(1)} %copy.42), channel_id=1, source_target_pairs={{0,1},{1,0},{2,3},{3,2},{4,5},{5,4},{6,7},{7,6},{8,9},{9,8},{10,11... | collective-permute-start | bytes 2211848 | tf_op jit(solution)/shard_map/ppermute | solution.py:149

commit v2 on v1

v2 whole, which is shorter than its diff:
```python
import jax
import jax.numpy as jnp
from jax import lax
from jax.experimental import pallas as pl
from jax.experimental.pallas import tpu as pltpu
from jax.sharding import Mesh
from jax.sharding import PartitionSpec as P

QUERY_HEADS = 32
KV_HEADS = 4
HEAD = 64
WINDOW = 128
KEYF = 256
GROUP = QUERY_HEADS // KV_HEADS
ROWS = 64
rope_base = 150000.0
masked_score = -1e30
bf16 = jnp.bfloat16
f32 = jnp.float32

DP = ("zl", "y")
CTX = ("zh", "x", "core")
Z = ("zl", "zh")
YX = ("y", "x")


def nt(a, b):
    return lax.dot_general(a, b, (((1,), (1,)), ((), ())), preferred_element_type=f32)


def nn(a, b):
    return lax.dot_general(a, b, (((1,), (0,)), ((), ())), preferred_element_type=f32)


def tn(a, b):
    return lax.dot_general(a, b, (((0,), (0,)), ((), ())), preferred_element_type=f32)


def swap_halves(x):
    lane = lax.broadcasted_iota(jnp.int32, x.shape, 1)
    width = x.shape[1]
    return jnp.where(lane % HEAD < HEAD // 2, pltpu.roll(x, width - HEAD // 2, 1), pltpu.roll(x, HEAD // 2, 1))


def project_kernel(tokens_ref, weight_ref, v_ref, cos_ref, sin_ref, keys_ref, edge_ref, packed_ref):
    parts, rows, wide = packed_ref.shape
    width = wide // parts
    linear = jnp.zeros((rows, KEYF), f32)
    for y in range(parts):
        for zl in range(parts):
            at = (zl * parts + y) * width
            packed_ref[y, :, zl * width : (zl + 1) * width] = tokens_ref[:, at : at + width]
        linear += nt(packed_ref[y], weight_ref[y])
    keys = (linear * cos_ref[...] + swap_halves(linear) * sin_ref[...]).astype(bf16)
    keys_ref[...] = keys
    edge_ref[0] = keys[rows - WINDOW :]
    edge_ref[1] = v_ref[rows - WINDOW :, :]


def attention_kernel(
    q_ref, g_ref, k_ref, v_ref, edge_ref, qd_ref, kd_ref,
    dq_ref, dk_ref, dv_ref, out_edge_ref,
    bias_ref, kk_ref, vv_ref, dka_ref, dva_ref,
):
    rows = q_ref.shape[0]
    span = ROWS + WINDOW
    lanes = GROUP * ROWS
    blocks = rows // ROWS

    @pl.when(pl.program_id(0) == 0)
    def _():
        key_at = lax.broadcasted_iota(jnp.int32, (span, lanes), 0)
        query_at = lax.broadcasted_iota(jnp.int32, (span, lanes), 1) % ROWS
        distance = query_at + WINDOW - key_at
        near = (distance >= 0) & (distance <= WINDOW)
        for b in range(blocks):
            same = kd_ref[b * ROWS : b * ROWS + span, :] == qd_ref[b]
            bias_ref[b] = jnp.where(near & same, 0.0, masked_score)

    lane = lax.broadcasted_iota(jnp.int32, (ROWS, 2 * HEAD), 1)
    low = jnp.where(lane < HEAD, 1.0, 0.0).astype(bf16)
    high = jnp.where(lane < HEAD, 0.0, 1.0).astype(bf16)

    def doubled(tile, head, scale):
        wide = tile.astype(f32) * scale
        at = lax.broadcasted_iota(jnp.int32, wide.shape, 1)
        return jnp.where(at // HEAD == head, wide, pltpu.roll(wide, HEAD, 1)).astype(bf16)

    def stacked(ref, b, head):
        parts = []
        for p in range(GROUP // 2):
            at = (head * GROUP // 2 + p) * 2 * HEAD
            pair = ref[b * ROWS : (b + 1) * ROWS, at : at + 2 * HEAD]
            parts += [pair * low, pair * high]
        return jnp.concatenate(parts, axis=0)

    for head in range(2):
        kk_ref[:WINDOW, :] = doubled(edge_ref[0], head, 0.125)
        kk_ref[WINDOW:, :] = doubled(k_ref[...], head, 0.125)
        vv_ref[:WINDOW, :] = doubled(edge_ref[1], head, 1.0)
        vv_ref[WINDOW:, :] = doubled(v_ref[...], head, 1.0)
        dka_ref[head] = jnp.zeros_like(dka_ref[head])
        dva_ref[head] = jnp.zeros_like(dva_ref[head])
        for b in range(blocks):
            band = slice(b * ROWS, b * ROWS + span)
            keys = kk_ref[band, :]
            values = vv_ref[band, :]
            qs = stacked(q_ref, b, head)
            gs = stacked(g_ref, b, head)
            scores = nt(keys, qs) + bias_ref[b]
            weights = jnp.exp(scores - jnp.max(scores, axis=0, keepdims=True))
            probs = weights * (1.0 / jnp.sum(weights, axis=0, keepdims=True))
            probs_low = probs.astype(bf16)
            prob_grad = nt(values, gs)
            delta = jnp.sum(probs_low.astype(f32) * prob_grad, axis=0, keepdims=True)
            score_low = (probs * (prob_grad - delta)).astype(bf16)
            dva_ref[head, band, :] += nn(probs_low, gs)
            dka_ref[head, band, :] += nn(score_low, qs)
            dq = tn(score_low, keys)
            for p in range(GROUP // 2):
                at = (head * GROUP // 2 + p) * 2 * HEAD
                top = dq[2 * p * ROWS : (2 * p + 1) * ROWS]
                bottom = dq[(2 * p + 1) * ROWS : (2 * p + 2) * ROWS]
                dq_ref[b * ROWS : (b + 1) * ROWS, at : at + 2 * HEAD] = jnp.where(
                    lane < HEAD, top, bottom
                ).astype(bf16)

    def joined(ref):
        first, second = ref[0], ref[1]
        at = lax.broadcasted_iota(jnp.int32, first.shape, 1)
        first = first + pltpu.roll(first, HEAD, 1)
        second = second + pltpu.roll(second, HEAD, 1)
        return jnp.where(at < HEAD, first, second)

    dk = joined(dka_ref) * 0.125
    dv = joined(dva_ref)
    out_edge_ref[0] = dk[:WINDOW].astype(bf16)
    out_edge_ref[1] = dv[:WINDOW].astype(bf16)
    dk_ref[...] = dk[WINDOW:]
    dv_ref[...] = dv[WINDOW:]


def tail_kernel(
    dk_ref, dv_ref, edge_ref, cos_ref, sin_ref, packed_ref, weight_ref, order_ref,
    vg_ref, ig_ref, own_ref, send_ref,
):
    parts, rows, wide = packed_ref.shape
    width = wide // parts
    start = rows - WINDOW
    vg_ref[:start, :] = dv_ref[:start, :].astype(bf16)
    vg_ref[start:, :] = (dv_ref[start:, :] + edge_ref[1].astype(f32)).astype(bf16)
    dk = jnp.concatenate([dk_ref[:start, :], dk_ref[start:, :] + edge_ref[0].astype(f32)], axis=0)
    lin = (dk * cos_ref[...] - swap_halves(dk) * sin_ref[...]).astype(bf16)
    ordered = nt(order_ref[...], lin).astype(bf16)
    half = KEYF // 2
    for y in range(parts):
        own_ref[y] = nn(ordered[:half], packed_ref[y])
        send_ref[y] = nn(ordered[half:], packed_ref[y]).astype(bf16)
        part = nn(lin, weight_ref[y]).astype(bf16)
        for zl in range(parts):
            at = (zl * parts + y) * width
            ig_ref[:, at : at + width] = part[:, zl * width : (zl + 1) * width]


def spread(x, axes):
    peers = lax.axis_size(axes)
    return lax.all_to_all(jnp.broadcast_to(x[None], (peers,) + x.shape), axes, 0, 0, tiled=True)


def exchanged(x, axis):
    return lax.ppermute(x, axis, [(0, 1), (1, 0)])


def gathered_weight(block):
    width, sub = block.shape
    zl, y, zh, x = (lax.axis_size(a) for a in ("zl", "y", "zh", "x"))
    along_z = spread(block.T, Z).reshape(zl, zh, sub, width)
    rows = along_z.transpose(1, 2, 0, 3).reshape(zh * sub, zl * width)
    mine = spread(rows, YX)
    other = exchanged(mine, "core")
    first = lax.axis_index("core") == 0
    pair = jnp.stack([jnp.where(first, mine, other), jnp.where(first, other, mine)])
    pair = pair.reshape(2, y, x, zh, sub, zl * width).transpose(1, 3, 2, 0, 4, 5)
    return pair.reshape(y, zh * x * 2 * sub, zl * width)


def summed(x, axes):
    return jnp.sum(lax.all_to_all(x, axes, 0, 0, tiled=True).astype(f32), axis=0)


def scattered_gradient(own, send, width, sub):
    zl, y, zh, x = (lax.axis_size(a) for a in ("zl", "y", "zh", "x"))
    both = (own + exchanged(send, "core").astype(f32)).astype(bf16)
    over_yx = summed(both.reshape(y * x, zh * sub, zl * width), YX).astype(bf16)
    over_yx = over_yx.reshape(zh, sub, zl, width).transpose(2, 0, 1, 3)
    return summed(over_yx.reshape(zl * zh, sub, width), Z)


def per_device(tokens_in, queries, values_in, key_weight, out_grad, doc_ids):
    rows = tokens_in.shape[1]
    dim = tokens_in.shape[2]
    width, sub = key_weight.shape
    tokens, q, g, v = tokens_in[0], queries[0], out_grad[0], values_in[0]
    q = pltpu.with_memory_space_constraint(q, pltpu.HBM)
    g = pltpu.with_memory_space_constraint(g, pltpu.HBM)
    blocks = rows // ROWS
    parts = lax.axis_size("y")
    peers = lax.axis_size(CTX)
    position = lax.axis_index(CTX)
    first_row = position * rows

    exponent = jnp.arange(HEAD // 2, dtype=f32) * (-2.0 / HEAD)
    inverse_freq = jnp.power(f32(rope_base), exponent)
    angles = (first_row + jnp.arange(rows, dtype=jnp.int32)).astype(f32)[:, None] * inverse_freq[None, :]
    cosine, sine = jnp.cos(angles), jnp.sin(angles)
    cos_table = jnp.tile(cosine, (1, 2 * KV_HEADS))
    sin_table = jnp.tile(jnp.concatenate([-sine, sine], axis=1), (1, KV_HEADS))

    padded_docs = jnp.concatenate([jnp.full((WINDOW,), -1, jnp.int32), doc_ids[0]])
    band_docs = lax.dynamic_slice_in_dim(padded_docs, first_row, rows + WINDOW)
    query_docs = jnp.tile(band_docs[WINDOW:].reshape(blocks, 1, ROWS), (1, 1, GROUP))
    key_docs = band_docs[:, None]

    core = lax.axis_index("core")
    dest = jnp.arange(KEYF, dtype=jnp.int32)
    rel, dest_x, dest_zh, dest_j = dest // 128, dest // 32 % 4, dest // 8 % 4, dest % 8
    source = dest_zh * 64 + dest_x * 16 + (rel ^ core) * 8 + dest_j
    order = (source[:, None] == jnp.arange(KEYF, dtype=jnp.int32)[None, :]).astype(bf16)

    weight = gathered_weight(key_weight)

    params = pltpu.CompilerParams(vmem_limit_bytes=24 << 20)
    keys, edge, packed = pl.pallas_call(
        project_kernel,
        out_shape=[
            jax.ShapeDtypeStruct((rows, KEYF), bf16),
            jax.ShapeDtypeStruct((2, WINDOW, KEYF), bf16),
            jax.ShapeDtypeStruct((parts, rows, dim // parts), bf16),
        ],
        compiler_params=params,
        name="project",
    )(tokens, weight, v, cos_table, sin_table)

    along = [(i, i + 1) for i in range(peers - 1)]
    back = [(i + 1, i) for i in range(peers - 1)]
    prior = lax.ppermute(edge, CTX, along)

    span = ROWS + WINDOW
    pair = 2 * HEAD
    heads = pl.BlockSpec((rows, 2 * GROUP * HEAD), lambda k: (0, k))
    own_tile = pl.BlockSpec((rows, pair), lambda k: (0, k))
    edge_tile = pl.BlockSpec((2, WINDOW, pair), lambda k: (0, 0, k))
    dq, dk, dv, out_edge = pl.pallas_call(
        attention_kernel,
        grid=(KV_HEADS // 2,),
        in_specs=[
            heads,
            heads,
            own_tile,
            own_tile,
            edge_tile,
            pl.BlockSpec((blocks, 1, GROUP * ROWS), lambda k: (0, 0, 0)),
            pl.BlockSpec((rows + WINDOW, 1), lambda k: (0, 0)),
        ],
        out_specs=[heads, own_tile, own_tile, edge_tile],
        out_shape=[
            jax.ShapeDtypeStruct((rows, QUERY_HEADS * HEAD), bf16),
            jax.ShapeDtypeStruct((rows, KEYF), f32),
            jax.ShapeDtypeStruct((rows, KEYF), f32),
            jax.ShapeDtypeStruct((2, WINDOW, KEYF), bf16),
        ],
        scratch_shapes=[
            pltpu.VMEM((blocks, span, GROUP * ROWS), f32),
            pltpu.VMEM((rows + WINDOW, pair), bf16),
            pltpu.VMEM((rows + WINDOW, pair), bf16),
            pltpu.VMEM((2, rows + WINDOW, pair), f32),
            pltpu.VMEM((2, rows + WINDOW, pair), f32),
        ],
        compiler_params=params,
        name="band_attention",
    )(q, g, keys, v, prior, query_docs, key_docs)

    incoming = lax.ppermute(out_edge, CTX, back)

    value_grad, input_grad, own, send = pl.pallas_call(
        tail_kernel,
        out_shape=[
            jax.ShapeDtypeStruct((rows, KEYF), bf16),
            jax.ShapeDtypeStruct((rows, dim), bf16),
            jax.ShapeDtypeStruct((parts, KEYF // 2, dim // parts), f32),
            jax.ShapeDtypeStruct((parts, KEYF // 2, dim // parts), bf16),
        ],
        compiler_params=params,
        name="tail",
    )(dk, dv, incoming, cos_table, sin_table, packed, weight, order)

    weight_grad = scattered_gradient(own, send, width, sub).T
    return dq[None], value_grad[None], input_grad[None], weight_grad


def solution(mesh):
    fine = Mesh(mesh.devices.reshape(4, 4, 4, 4, 2), ("zl", "y", "zh", "x", "core"))
    rows = P(DP, CTX, None)
    square = P(DP, CTX)
    return jax.shard_map(
        per_device,
        mesh=fine,
        in_specs=(rows, rows, rows, square, rows, P(DP, None)),
        out_specs=(rows, rows, rows, square),
        check_vma=False,
    )
```

time: 159 us -> 138 us (0.87)
  waiting for transfers between devices: 14 us -> 6.93 us
  starting transfers between devices: 17 us -> 11.4 us
  local copies, waits for them, and re-layouts: 11 us -> 6.58 us
  blocking collectives: 102 us -> 98.7 us
    all_to_all x1 -> x2, blocking collectives: 27.2 us -> 47 us  [spread(): lax.all_to_all(jnp.broadcast_to(x[None], (peers,) + x.shape), axes, 0, 0,...]
    all_gather x1 -> x0, blocking collectives: 14.3 us -> none  [gathered_weight(): along_x = lax.all_gather(rows, 'x', axis=0)]
    all_to_all x3 -> x2, blocking collectives: 60.7 us -> 51.6 us  [summed(): lax.all_to_all(x, axes, 0, 0, tiled=True).astype(f32)]
    all_to_all x1 -> x0, waiting for transfers between devices: 6.68 us -> none  [spread(): lax.all_to_all(jnp.broadcast_to(x[None], (peers,) + x.shape), axes, 0, 0,...]
    all_to_all x1 -> x0, starting transfers between devices: 4.46 us -> none  [spread(): lax.all_to_all(jnp.broadcast_to(x[None], (peers,) + x.shape), axes, 0, 0,...]
    unnamed x16 -> x12, local copies, waits for them, and re-layouts: 5.44 us -> 2.97 us
  transfers between devices with their start and end apart: 5 -> 4, of which waited for: 5 -> 4; matrix products, arithmetic and copies ran while one was open for 1% -> 1% of each run, Pallas kernels for 0% -> 0%
where the time goes in v2:
time: 138 us; the launch traced here: 137 us
  blocking collectives  98.7 us (72%)
  starting transfers between devices  11.4 us (8%)
  Pallas kernels  11.4 us (8%)
  waiting for transfers between devices  6.93 us (5%)
  local copies, waits for them, and re-layouts  6.58 us (5%)
  other arithmetic  1.5 us (1%)
    all_to_all x2, blocking collectives, summed(): lax.all_to_all(x, axes, 0, 0, tiled=True).astype(f32)  51.6 us
    all_to_all x2, blocking collectives, spread(): lax.all_to_all(jnp.broadcast_to(x[None], (peers,) + x.shape), axes, 0, 0,...  47 us
    pallas_call x1, Pallas kernels, per_device(): pl.pallas_call(attention_kernel, grid=(KV_HEADS // 2,), in_specs=[heads,...  8.13 us
    ppermute x2, starting transfers between devices, exchanged(): return lax.ppermute(x, axis, [(0, 1), (1, 0)])  8.07 us
    ppermute x2, waiting for transfers between devices, exchanged(): return lax.ppermute(x, axis, [(0, 1), (1, 0)])  3.52 us
    unnamed x12, local copies, waits for them, and re-layouts  2.97 us
    ppermute x1, waiting for transfers between devices, per_device(): incoming = lax.ppermute(out_edge, CTX, back)  2.84 us
  transfers between devices with their start and end apart: 4, of which 4 were waited for; matrix products, arithmetic and copies ran while one was open for 1% of the time, Pallas kernels for 0%

profile of v2, /device:TPU:32, one launch (start us, length us, event | category | flops | bytes accessed | tf_op | source)
XLA Modules:
  0.0 137.4 jit_solution(6376483791272258307)
XLA Ops:
  0.6 0.7 broadcast_in_dim.14
  1.3 27.2 %all_to_all.20 = bf16[16,8,180]{2,1,0:T(8,128)(2,1)S(1)} all-to-all(bf16[16,8,180]{2,1,0:T(8,128)(2,1)S(1)} %broadcast_in_dim.14), channel_id=1, replica_groups=mesh['zl'=4,'y'=4,'zh'=4,'x'=4,'core'=2] {'zl','zh'}, dimensions={0} | all-to-all | bytes 92160 | tf_op jit(solution)/shard_map/all_to_all | solution.py:167
  28.5 0.1 copy.24
  28.5 0.1 broadcast_in_dim.15
  28.6 0.1 broadcast_in_dim.32
  28.7 19.9 %all_to_all.21 = bf16[16,32,720]{2,1,0:T(8,128)(2,1)S(1)} all-to-all(bf16[16,32,720]{2,1,0:T(8,128)(2,1)S(1)} %broadcast_in_dim.32), channel_id=1, replica_groups=mesh['zl'=4,'y'=4,'zh'=4,'x'=4,'core'=2] {'y','x'}, dimensions={0} | all-to-all | bytes 1474560 | tf_op jit(solution)/shard_map/all_to_all | solution.py:167
  48.6 1.9 %collective-permute-start = (bf16[16,32,720]{2,1,0:T(8,128)(2,1)S(1)}, bf16[16,32,720]{2,1,0:T(8,128)(2,1)S(1)}, u32[]{:S(2)}, u32[]{:S(2)}) collective-permute-start(bf16[16,32,720]{2,1,0:T(8,128)(2,1)S(1)} %all_to_all.21), channel_id=1, source_target_pairs={{0,1},{1,0},{2,3},{3,2},{4,5},{5,4},{6,7},{7,6},{8,9},{9,8},{10,11... | collective-permute-start | bytes 2211848 | tf_op jit(solution)/shard_map/ppermute | solution.py:171
  50.6 0.2 fusion.1
  50.8 0.1 copy.27.sin_ref
  51.0 0.1 copy.26.cos_ref
  51.1 1.7 %collective-permute-done = bf16[16,32,720]{2,1,0:T(8,128)(2,1)S(1)} collective-permute-done((bf16[16,32,720]{2,1,0:T(8,128)(2,1)S(1)}, bf16[16,32,720]{2,1,0:T(8,128)(2,1)S(1)}, u32[]{:S(2)}, u32[]{:S(2)}) %collective-permute-start) | collective-permute-done | bytes 737312 | tf_op jit(solution)/shard_map/ppermute | solution.py:171
  52.8 0.1 broadcast_select_fusion.1
  52.9 0.2 maximum_bitcast_fusion
  53.0 0.0 copy-start.2
  53.1 0.0 copy-start.4
  53.1 0.2 copy.25
  53.2 1.1 copy-done.2
  54.3 0.0 copy-done.4
  54.3 0.0 copy-start.5
  54.3 1.0 project.1
  55.3 0.0 copy-start
  55.3 1.0 copy-done
  56.4 2.0 %collective-permute-start.1 = (bf16[2,128,256]{2,1,0:T(8,128)(2,1)S(1)}, bf16[2,128,256]{2,1,0:T(8,128)(2,1)S(1)}, u32[]{:S(2)}, u32[]{:S(2)}) collective-permute-start(bf16[2,128,256]{2,1,0:T(8,128)(2,1)S(1)} %get-tuple-element.16), channel_id=1, source_target_pairs={{0,1},{1,2},{2,3},{3,4},{4,5},{5,6},{6,7},{7,8},{8,9},{9,10},{10,1... | collective-permute-start | bytes 393224 | tf_op jit(solution)/shard_map/ppermute | solution.py:246
  58.4 0.0 copy-done.5
  58.4 0.1 pad_dynamic-slice_fusion
  58.5 0.1 broadcast_in_dim.37.kd_ref
  58.6 0.1 tile.32
  58.7 0.1 tile.34.qd_ref
  58.8 0.0 copy-start.1
  58.8 0.6 collective-permute-done.1.edge_ref
  59.4 8.1 %band_attention.1 = (bf16[192,2048]{1,0:T(8,128)(2,1)}, f32[192,256]{1,0:T(8,128)S(1)}, f32[192,256]{1,0:T(8,128)S(1)}, bf16[2,128,256]{2,1,0:T(8,128)(2,1)S(1)}) custom-call(bf16[192,2048]{1,0:T(8,128)(2,1)} %bitcast.33, bf16[192,2048]{1,0:T(8,128)(2,1)} %bitcast.34, bf16[192,256]{1,0:T(8,128)(2,1)S(1)} %get-tuple-element.15.k_ref, ...), custom_call_target="tpu_custom_call" | custom-call | tf_op jit(solution)/shard_map/band_attention/pallas_call | solution.py:253
  67.5 1.3 collective-permute-start.2
  68.8 0.1 fusion.order_ref
  68.9 2.8 %collective-permute-done.2.edge_ref = bf16[2,128,256]{2,1,0:T(8,128)(2,1)S(1)} collective-permute-done((bf16[2,128,256]{2,1,0:T(8,128)(2,1)S(1)}, bf16[2,128,256]{2,1,0:T(8,128)(2,1)S(1)}, u32[]{:S(2)}, u32[]{:S(2)}) %collective-permute-start.2) | collective-permute-done | bytes 131104 | tf_op jit(solution)/shard_map/ppermute | solution.py:283
  71.7 0.0 copy-done.1
  71.7 2.3 %tail.1 = (bf16[192,256]{1,0:T(8,128)(2,1)}, bf16[192,2880]{1,0:T(8,128)(2,1)}, f32[4,128,720]{2,1,0:T(8,128)S(1)}, bf16[4,128,720]{2,1,0:T(8,128)(2,1)S(1)}) custom-call(f32[192,256]{1,0:T(8,128)S(1)} %get-tuple-element.18.dk_ref, f32[192,256]{1,0:T(8,128)S(1)} %get-tuple-element.19.dv_ref, bf16[2,128,256]{2,1,0:T(8,128)(2,1)S(1)} %collective-permute-done.2.edge_ref, ...), custom_call_target="tpu_custom_call" | custom-call | tf_op jit(solution)/shard_map/tail/pallas_call | solution.py:285
  74.0 0.0 copy-start.3
  74.0 0.9 copy-done.3
  74.9 1.5 %copy.31 = bf16[4,128,720]{1,2,0:T(8,128)(2,1)S(1)} copy(bf16[4,128,720]{2,1,0:T(8,128)(2,1)} %copy-done.3) | data formatting | bytes 1474560 | tf_op jit(solution)/shard_map/tail/pallas_call | solution.py:285
  76.4 6.2 %collective-permute-start.3 = (bf16[4,128,720]{1,2,0:T(8,128)(2,1)S(1)}, bf16[4,128,720]{1,2,0:T(8,128)(2,1)S(1)}, u32[]{:S(2)}, u32[]{:S(2)}) collective-permute-start(bf16[4,128,720]{1,2,0:T(8,128)(2,1)S(1)} %copy.31), channel_id=1, source_target_pairs={{0,1},{1,0},{2,3},{3,2},{4,5},{5,4},{6,7},{7,6},{8,9},{9,8},{10,11... | collective-permute-start | bytes 2211848 | tf_op jit(solution)/shard_map/ppermute | solution.py:171
  82.6 1.8 %collective-permute-done.3 = bf16[4,128,720]{1,2,0:T(8,128)(2,1)S(1)} collective-permute-done((bf16[4,128,720]{1,2,0:T(8,128)(2,1)S(1)}, bf16[4,128,720]{1,2,0:T(8,128)(2,1)S(1)}, u32[]{:S(2)}, u32[]{:S(2)}) %collective-permute-start.3) | collective-permute-done | bytes 737312 | tf_op jit(solution)/shard_map/ppermute | solution.py:171
  84.4 0.3 copy.32
  84.7 0.2 add_convert_fusion
  84.9 28.8 %all_to_all.22 = bf16[16,32,720]{2,1,0:T(8,128)(2,1)S(1)} all-to-all(bf16[16,32,720]{2,1,0:T(8,128)(2,1)S(1)} %bitcast.28), channel_id=1, replica_groups=mesh['zl'=4,'y'=4,'zh'=4,'x'=4,'core'=2] {'y','x'}, dimensions={0} | all-to-all | bytes 1474560 | tf_op jit(solution)/shard_map/all_to_all | solution.py:188
  113.7 0.1 reduce_sum.21
  113.8 0.1 reshape.154
  113.9 22.8 %all_to_all.23 = bf16[16,8,180]{2,1,0:T(8,128)(2,1)S(1)} all-to-all(bf16[16,8,180]{2,1,0:T(8,128)(2,1)S(1)} %bitcast.37), channel_id=1, replica_groups=mesh['zl'=4,'y'=4,'zh'=4,'x'=4,'core'=2] {'zl','zh'}, dimensions={0} | all-to-all | bytes 92160 | tf_op jit(solution)/shard_map/all_to_all | solution.py:188
  136.8 0.6 convert_reduce_fusion
  (9 shorter events, 0.1 us)
Async XLA Ops:
  48.6 4.2 %collective-permute-start = (bf16[16,32,720]{2,1,0:T(8,128)(2,1)S(1)}, bf16[16,32,720]{2,1,0:T(8,128)(2,1)S(1)}, u32[]{:S(2)}, u32[]{:S(2)}) collective-permute-start(bf16[16,32,720]{2,1,0:T(8,128)(2,1)S(1)} %all_to_all.21), channel_id=1, source_target_pairs={{0,1},{1,0},{2,3},{3,2},{4,5},{5,4},{6,7},{7,6},{8,9},{9,8},{10,11... | collective-permute-start | bytes 2211848 | tf_op jit(solution)/shard_map/ppermute | solution.py:171
  53.0 1.3 copy-start.2
  53.1 1.2 copy-start.4
  54.3 4.1 %copy-start.5 = (s32[1,6144]{1,0:T(1,128)S(1)}, s32[1,6144]{1,0:T(1,128)}, u32[]{:S(2)}) copy-start(s32[1,6144]{1,0:T(1,128)} %param.11) | copy-start | bytes 73732
  55.3 1.0 copy-start
  56.4 3.0 %collective-permute-start.1 = (bf16[2,128,256]{2,1,0:T(8,128)(2,1)S(1)}, bf16[2,128,256]{2,1,0:T(8,128)(2,1)S(1)}, u32[]{:S(2)}, u32[]{:S(2)}) collective-permute-start(bf16[2,128,256]{2,1,0:T(8,128)(2,1)S(1)} %get-tuple-element.16), channel_id=1, source_target_pairs={{0,1},{1,2},{2,3},{3,4},{4,5},{5,6},{6,7},{7,8},{8,9},{9,10},{10,1... | collective-permute-start | bytes 393224 | tf_op jit(solution)/shard_map/ppermute | solution.py:246
  58.8 13.0 %copy-start.1 = (bf16[4,192,720]{2,1,0:T(8,128)(2,1)S(1)}, bf16[4,192,720]{2,1,0:T(8,128)(2,1)}, u32[]{:S(2)}) copy-start(bf16[4,192,720]{2,1,0:T(8,128)(2,1)} %copy-done) | copy-start | bytes 3317764
  67.5 4.2 %collective-permute-start.2 = (bf16[2,128,256]{2,1,0:T(8,128)(2,1)S(1)}, bf16[2,128,256]{2,1,0:T(8,128)(2,1)S(1)}, u32[]{:S(2)}, u32[]{:S(2)}) collective-permute-start(bf16[2,128,256]{2,1,0:T(8,128)(2,1)S(1)} %get-tuple-element.20), channel_id=1, source_target_pairs={{1,0},{2,1},{3,2},{4,3},{5,4},{6,5},{7,6},{8,7},{9,8},{10,9},{11,1... | collective-permute-start | bytes 393224 | tf_op jit(solution)/shard_map/ppermute | solution.py:283
  74.0 0.9 copy-start.3
  76.4 8.0 %collective-permute-start.3 = (bf16[4,128,720]{1,2,0:T(8,128)(2,1)S(1)}, bf16[4,128,720]{1,2,0:T(8,128)(2,1)S(1)}, u32[]{:S(2)}, u32[]{:S(2)}) collective-permute-start(bf16[4,128,720]{1,2,0:T(8,128)(2,1)S(1)} %copy.31), channel_id=1, source_target_pairs={{0,1},{1,0},{2,3},{3,2},{4,5},{5,4},{6,7},{7,6},{8,9},{9,8},{10,11... | collective-permute-start | bytes 2211848 | tf_op jit(solution)/shard_map/ppermute | solution.py:171

commit v3 on v2

--- a/solution.py
+++ b/solution.py
@@ -42,14 +42,20 @@
     return jnp.where(lane % HEAD < HEAD // 2, pltpu.roll(x, width - HEAD // 2, 1), pltpu.roll(x, HEAD // 2, 1))
 
 
-def project_kernel(tokens_ref, weight_ref, v_ref, cos_ref, sin_ref, keys_ref, edge_ref, packed_ref):
-    parts, rows, wide = packed_ref.shape
+def pack(tokens_ref, packed_ref):
+    parts, _, wide = packed_ref.shape
     width = wide // parts
-    linear = jnp.zeros((rows, KEYF), f32)
     for y in range(parts):
         for zl in range(parts):
             at = (zl * parts + y) * width
             packed_ref[y, :, zl * width : (zl + 1) * width] = tokens_ref[:, at : at + width]
+
+
+def project_kernel(tokens_ref, weight_ref, v_ref, cos_ref, sin_ref, keys_ref, edge_ref, packed_ref):
+    parts, rows, _ = packed_ref.shape
+    pack(tokens_ref, packed_ref)
+    linear = jnp.zeros((rows, KEYF), f32)
+    for y in range(parts):
         linear += nt(packed_ref[y], weight_ref[y])
     keys = (linear * cos_ref[...] + swap_halves(linear) * sin_ref[...]).astype(bf16)
     keys_ref[...] = keys
@@ -57,15 +63,10 @@
     edge_ref[1] = v_ref[rows - WINDOW :, :]
 
 
-def attention_kernel(
-    q_ref, g_ref, k_ref, v_ref, edge_ref, qd_ref, kd_ref,
-    dq_ref, dk_ref, dv_ref, out_edge_ref,
-    bias_ref, kk_ref, vv_ref, dka_ref, dva_ref,
-):
-    rows = q_ref.shape[0]
+def band_pairs(q_ref, g_ref, qd_ref, kd_ref, dq_ref, bias_ref, kk_ref, vv_ref, dka_ref, dva_ref, fill):
+    blocks = q_ref.shape[0] // ROWS
     span = ROWS + WINDOW
     lanes = GROUP * ROWS
-    blocks = rows // ROWS
 
     @pl.when(pl.program_id(0) == 0)
     def _():
@@ -81,11 +82,6 @@
     low = jnp.where(lane < HEAD, 1.0, 0.0).astype(bf16)
     high = jnp.where(lane < HEAD, 0.0, 1.0).astype(bf16)
 
-    def doubled(tile, head, scale):
-        wide = tile.astype(f32) * scale
-        at = lax.broadcasted_iota(jnp.int32, wide.shape, 1)
-        return jnp.where(at // HEAD == head, wide, pltpu.roll(wide, HEAD, 1)).astype(bf16)
-
     def stacked(ref, b, head):
         parts = []
         for p in range(GROUP // 2):
@@ -95,10 +91,7 @@
         return jnp.concatenate(parts, axis=0)
 
     for head in range(2):
-        kk_ref[:WINDOW, :] = doubled(edge_ref[0], head, 0.125)
-        kk_ref[WINDOW:, :] = doubled(k_ref[...], head, 0.125)
-        vv_ref[:WINDOW, :] = doubled(edge_ref[1], head, 1.0)
-        vv_ref[WINDOW:, :] = doubled(v_ref[...], head, 1.0)
+        fill(head)
         dka_ref[head] = jnp.zeros_like(dka_ref[head])
         dva_ref[head] = jnp.zeros_like(dva_ref[head])
         for b in range(blocks):
@@ -132,34 +125,85 @@
         second = second + pltpu.roll(second, HEAD, 1)
         return jnp.where(at < HEAD, first, second)
 
-    dk = joined(dka_ref) * 0.125
-    dv = joined(dva_ref)
+    return joined(dka_ref) * 0.125, joined(dva_ref)
+
+
+def doubled(tile, head, scale):
+    wide = tile.astype(f32) * scale
+    at = lax.broadcasted_iota(jnp.int32, wide.shape, 1)
+    return jnp.where(at // HEAD == head, wide, pltpu.roll(wide, HEAD, 1)).astype(bf16)
+
+
+def early_kernel(
+    q_ref, g_ref, k_ref, v_ref, edge_ref, qd_ref, kd_ref,
+    dq_ref, dk_ref, dv_ref, out_edge_ref,
+    bias_ref, kk_ref, vv_ref, dka_ref, dva_ref,
+):
+    def fill(head):
+        kk_ref[:WINDOW, :] = doubled(edge_ref[0], head, 0.125)
+        kk_ref[WINDOW:, :] = doubled(k_ref[...], head, 0.125)
+        vv_ref[:WINDOW, :] = doubled(edge_ref[1], head, 1.0)
+        vv_ref[WINDOW:, :] = doubled(v_ref[...], head, 1.0)
+
+    dk, dv = band_pairs(q_ref, g_ref, qd_ref, kd_ref, dq_ref, bias_ref, kk_ref, vv_ref, dka_ref, dva_ref, fill)
     out_edge_ref[0] = dk[:WINDOW].astype(bf16)
     out_edge_ref[1] = dv[:WINDOW].astype(bf16)
     dk_ref[...] = dk[WINDOW:]
     dv_ref[...] = dv[WINDOW:]
 
 
+def late_kernel(
+    q_ref, g_ref, k_ref, v_ref, qd_ref, kd_ref, _,
+    dq_ref, dk_ref, dv_ref,
+    bias_ref, kk_ref, vv_ref, dka_ref, dva_ref,
+):
+    def fill(head):
+        kk_ref[...] = doubled(k_ref[...], head, 0.125)
+        vv_ref[...] = doubled(v_ref[...], head, 1.0)
+
+    dk, dv = band_pairs(q_ref, g_ref, qd_ref, kd_ref, dq_ref, bias_ref, kk_ref, vv_ref, dka_ref, dva_ref, fill)
+    dk_ref[...] = dk
+    dv_ref[...] = dv
+
+
 def tail_kernel(
-    dk_ref, dv_ref, edge_ref, cos_ref, sin_ref, packed_ref, weight_ref, order_ref,
-    vg_ref, ig_ref, own_ref, send_ref,
+    dk1_ref, dv1_ref, dk2_ref, dv2_ref, edge_ref, cos_ref, sin_ref, tokens_ref, order_ref,
+    vg_ref, lin_ref, own_ref, send_ref, packed_ref,
 ):
     parts, rows, wide = packed_ref.shape
-    width = wide // parts
     start = rows - WINDOW
-    vg_ref[:start, :] = dv_ref[:start, :].astype(bf16)
-    vg_ref[start:, :] = (dv_ref[start:, :] + edge_ref[1].astype(f32)).astype(bf16)
-    dk = jnp.concatenate([dk_ref[:start, :], dk_ref[start:, :] + edge_ref[0].astype(f32)], axis=0)
+
+    def total(early_ref, late_ref, edge):
+        sums = late_ref[...]
+        sums = jnp.concatenate([sums[:WINDOW] + early_ref[...], sums[WINDOW:]], axis=0)
+        return jnp.concatenate([sums[:start], sums[start:] + edge.astype(f32)], axis=0)
+
+    vg_ref[...] = total(dv1_ref, dv2_ref, edge_ref[1]).astype(bf16)
+    dk = total(dk1_ref, dk2_ref, edge_ref[0])
     lin = (dk * cos_ref[...] - swap_halves(dk) * sin_ref[...]).astype(bf16)
+    lin_ref[...] = lin
     ordered = nt(order_ref[...], lin).astype(bf16)
     half = KEYF // 2
+    block = (parts, half // parts, wide)
+    pack(tokens_ref, packed_ref)
     for y in range(parts):
-        own_ref[y] = nn(ordered[:half], packed_ref[y])
-        send_ref[y] = nn(ordered[half:], packed_ref[y]).astype(bf16)
-        part = nn(lin, weight_ref[y]).astype(bf16)
+        to = slice(y * parts, (y + 1) * parts)
+        own_ref[to] = nn(ordered[:half], packed_ref[y]).reshape(block)
+        send_ref[to] = nn(ordered[half:], packed_ref[y]).reshape(block).astype(bf16)
+
+
+def input_kernel(lin_ref, weight_ref, ig_ref):
+    parts = weight_ref.shape[0]
+    width = weight_ref.shape[2] // parts
+    for y in range(parts):
+        part = nn(lin_ref[...], weight_ref[y]).astype(bf16)
         for zl in range(parts):
             at = (zl * parts + y) * width
             ig_ref[:, at : at + width] = part[:, zl * width : (zl + 1) * width]
+
+
+def room(mib):
+    return pltpu.CompilerParams(vmem_limit_bytes=mib << 20)
 
 
 def spread(x, axes):
@@ -188,12 +232,13 @@
     return jnp.sum(lax.all_to_all(x, axes, 0, 0, tiled=True).astype(f32), axis=0)
 
 
-def scattered_gradient(own, send, width, sub):
-    zl, y, zh, x = (lax.axis_size(a) for a in ("zl", "y", "zh", "x"))
-    both = (own + exchanged(send, "core").astype(f32)).astype(bf16)
-    over_yx = summed(both.reshape(y * x, zh * sub, zl * width), YX).astype(bf16)
+def scattered_gradient(own, send, beside, width, sub):
+    zl, zh = lax.axis_size("zl"), lax.axis_size("zh")
+    other, beside = lax.optimization_barrier((exchanged(send, "core"), beside))
+    both = (own + other.astype(f32)).astype(bf16)
+    over_yx = summed(both, YX).astype(bf16)
     over_yx = over_yx.reshape(zh, sub, zl, width).transpose(2, 0, 1, 3)
-    return summed(over_yx.reshape(zl * zh, sub, width), Z)
+    return summed(over_yx.reshape(zl * zh, sub, width), Z), beside
 
 
 def per_device(tokens_in, queries, values_in, key_weight, out_grad, doc_ids):
@@ -228,16 +273,11 @@
     order = (source[:, None] == jnp.arange(KEYF, dtype=jnp.int32)[None, :]).astype(bf16)
 
     weight = gathered_weight(key_weight)
-
-    params = pltpu.CompilerParams(vmem_limit_bytes=24 << 20)
-    keys, edge, packed = pl.pallas_call(
+    keys, edge = pl.pallas_call(
         project_kernel,
-        out_shape=[
-            jax.ShapeDtypeStruct((rows, KEYF), bf16),
-            jax.ShapeDtypeStruct((2, WINDOW, KEYF), bf16),
-            jax.ShapeDtypeStruct((parts, rows, dim // parts), bf16),
-        ],
-        compiler_params=params,
+        out_shape=[jax.ShapeDtypeStruct((rows, KEYF), bf16), jax.ShapeDtypeStruct((2, WINDOW, KEYF), bf16)],
+        scratch_shapes=[pltpu.VMEM((parts, rows, dim // parts), bf16)],
+        compiler_params=room(10),
         name="project",
     )(tokens, weight, v, cos_table, sin_table)
 
@@ -247,55 +287,99 @@
 
     span = ROWS + WINDOW
     pair = 2 * HEAD
-    heads = pl.BlockSpec((rows, 2 * GROUP * HEAD), lambda k: (0, k))
-    own_tile = pl.BlockSpec((rows, pair), lambda k: (0, k))
+    wide = 2 * GROUP * HEAD
     edge_tile = pl.BlockSpec((2, WINDOW, pair), lambda k: (0, 0, k))
-    dq, dk, dv, out_edge = pl.pallas_call(
-        attention_kernel,
+
+    def tile(size):
+        return pl.BlockSpec((size, pair), lambda k: (0, k))
+
+    def heads(size, at):
+        return pl.BlockSpec((size, wide), lambda k: (at, k))
+
+    def fixed(shape):
+        return pl.BlockSpec(shape, lambda k: (0,) * len(shape))
+
+    def scratch(count):
+        band = (count - 1) * ROWS + span
+        return [
+            pltpu.VMEM((count, span, GROUP * ROWS), f32),
+            pltpu.VMEM((band, pair), bf16),
+            pltpu.VMEM((band, pair), bf16),
+            pltpu.VMEM((2, band, pair), f32),
+            pltpu.VMEM((2, band, pair), f32),
+        ]
+
+    dq, dk1, dv1, out_edge = pl.pallas_call(
+        early_kernel,
         grid=(KV_HEADS // 2,),
         in_specs=[
-            heads,
-            heads,
-            own_tile,
-            own_tile,
+            heads(WINDOW, 0),
+            heads(WINDOW, 0),
+            tile(WINDOW),
+            tile(WINDOW),
             edge_tile,
-            pl.BlockSpec((blocks, 1, GROUP * ROWS), lambda k: (0, 0, 0)),
-            pl.BlockSpec((rows + WINDOW, 1), lambda k: (0, 0)),
-        ],
-        out_specs=[heads, own_tile, own_tile, edge_tile],
+            fixed((2, 1, GROUP * ROWS)),
+            fixed((2 * WINDOW, 1)),
+        ],
+        out_specs=[heads(WINDOW, 0), tile(WINDOW), tile(WINDOW), edge_tile],
+        out_shape=[
+            jax.ShapeDtypeStruct((rows, QUERY_HEADS * HEAD), bf16),
+            jax.ShapeDtypeStruct((WINDOW, KEYF), f32),
+            jax.ShapeDtypeStruct((WINDOW, KEYF), f32),
+            jax.ShapeDtypeStruct((2, WINDOW, KEYF), bf16),
+        ],
+        scratch_shapes=scratch(2),
+        compiler_params=room(16),
+        name="band_early",
+    )(q, g, keys, v, prior, query_docs[:2], key_docs[: 2 * WINDOW])
+
+    incoming = lax.ppermute(out_edge, CTX, back)
+
+    dq, dk2, dv2 = pl.pallas_call(
+        late_kernel,
+        grid=(KV_HEADS // 2,),
+        in_specs=[
+            heads(ROWS, 2),
+            heads(ROWS, 2),
+            tile(rows),
+            tile(rows),
+            fixed((1, 1, GROUP * ROWS)),
+            fixed((rows, 1)),
+            pl.BlockSpec(memory_space=pl.ANY),
+        ],
+        out_specs=[heads(ROWS, 2), tile(rows), tile(rows)],
         out_shape=[
             jax.ShapeDtypeStruct((rows, QUERY_HEADS * HEAD), bf16),
             jax.ShapeDtypeStruct((rows, KEYF), f32),
             jax.ShapeDtypeStruct((rows, KEYF), f32),
-            jax.ShapeDtypeStruct((2, WINDOW, KEYF), bf16),
-        ],
-        scratch_shapes=[
-            pltpu.VMEM((blocks, span, GROUP * ROWS), f32),
-            pltpu.VMEM((rows + WINDOW, pair), bf16),
-            pltpu.VMEM((rows + WINDOW, pair), bf16),
-            pltpu.VMEM((2, rows + WINDOW, pair), f32),
-            pltpu.VMEM((2, rows + WINDOW, pair), f32),
-        ],
-        compiler_params=params,
-        name="band_attention",
-    )(q, g, keys, v, prior, query_docs, key_docs)
-
-    incoming = lax.ppermute(out_edge, CTX, back)
-
-    value_grad, input_grad, own, send = pl.pallas_call(
+        ],
+        input_output_aliases={6: 0},
+        scratch_shapes=scratch(1),
+        compiler_params=room(16),
+        name="band_late",
+    )(q, g, keys, v, query_docs[2:], key_docs[WINDOW:], dq)
+
+    value_grad, lin, own, send = pl.pallas_call(
         tail_kernel,
         out_shape=[
             jax.ShapeDtypeStruct((rows, KEYF), bf16),
-            jax.ShapeDtypeStruct((rows, dim), bf16),
-            jax.ShapeDtypeStruct((parts, KEYF // 2, dim // parts), f32),
-            jax.ShapeDtypeStruct((parts, KEYF // 2, dim // parts), bf16),
-        ],
-        compiler_params=params,
+            jax.ShapeDtypeStruct((rows, KEYF), bf16),
+            jax.ShapeDtypeStruct((parts * parts, KEYF // 2 // parts, dim // parts), f32),
+            jax.ShapeDtypeStruct((parts * parts, KEYF // 2 // parts, dim // parts), bf16),
+        ],
+        scratch_shapes=[pltpu.VMEM((parts, rows, dim // parts), bf16)],
+        compiler_params=room(16),
         name="tail",
-    )(dk, dv, incoming, cos_table, sin_table, packed, weight, order)
-
-    weight_grad = scattered_gradient(own, send, width, sub).T
-    return dq[None], value_grad[None], input_grad[None], weight_grad
+    )(dk1, dv1, dk2, dv2, incoming, cos_table, sin_table, tokens, order)
+    input_grad = pl.pallas_call(
+        input_kernel,
+        out_shape=jax.ShapeDtypeStruct((rows, dim), bf16),
+        compiler_params=room(8),
+        name="input_grad",
+    )(lin, weight)
+
+    weight_grad, input_grad = scattered_gradient(own, send, input_grad, width, sub)
+    return dq[None], value_grad[None], input_grad[None], weight_grad.T
 
 
 def solution(mesh):

time: 138 us -> 134 us (0.971)
  waiting for transfers between devices: 6.93 us -> 1.98 us
  Pallas kernels: 11.4 us -> 15.3 us
  local copies, waits for them, and re-layouts: 6.58 us -> 3.13 us
    pallas_call x1 -> x3, Pallas kernels: 8.13 us -> 12 us  [the longest x1 6.12 us: per_device(): pl.pallas_call(early_kernel, grid=(KV_HEADS // 2,), in_specs=[heads(WINDO...]
    ppermute x1, waiting for transfers between devices: 2.84 us -> 0.01 us  [per_device(): incoming = lax.ppermute(out_edge, CTX, back)]
    unnamed x12 -> x6, local copies, waits for them, and re-layouts: 2.97 us -> 1.07 us
    ppermute x2, waiting for transfers between devices: 3.52 us -> 1.96 us  [exchanged(): return lax.ppermute(x, axis, [(0, 1), (1, 0)])]
    pallas_call x1 -> x0, local copies, waits for them, and re-layouts: 1.5 us -> none  [per_device(): pl.pallas_call(tail_kernel, out_shape=[jax.ShapeDtypeStruct((rows, KEYF),...]
  transfers between devices with their start and end apart: 4 -> 4, of which waited for: 4 -> 2; matrix products, arithmetic and copies ran while one was open for 1% -> 1% of each run, Pallas kernels for 0% -> 4%
where the time goes in v3:
time: 134 us; the launch traced here: 133 us
  blocking collectives  98.7 us (74%)
  Pallas kernels  15.3 us (11%)
  starting transfers between devices  10.7 us (8%)
  local copies, waits for them, and re-layouts  3.13 us (2%)
  other arithmetic  2.69 us (2%)
  waiting for transfers between devices  1.98 us (1%)
    all_to_all x2, blocking collectives, summed(): lax.all_to_all(x, axes, 0, 0, tiled=True).astype(f32)  51.6 us
    all_to_all x2, blocking collectives, spread(): lax.all_to_all(jnp.broadcast_to(x[None], (peers,) + x.shape), axes, 0, 0,...  47 us
    ppermute x2, starting transfers between devices, exchanged(): return lax.ppermute(x, axis, [(0, 1), (1, 0)])  6.72 us
    pallas_call x1, Pallas kernels, per_device(): pl.pallas_call(early_kernel, grid=(KV_HEADS // 2,), in_specs=[heads(WINDO...  6.12 us
    pallas_call x1, Pallas kernels, per_device(): pl.pallas_call(late_kernel, grid=(KV_HEADS // 2,), in_specs=[heads(ROWS,...  4.15 us
    ppermute x1, starting transfers between devices, per_device(): prior = lax.ppermute(edge, CTX, along)  2.69 us
  transfers between devices with their start and end apart: 4, of which 2 were waited for; matrix products, arithmetic and copies ran while one was open for 1% of the time, Pallas kernels for 4%

profile of v3, /device:TPU:32, one launch (start us, length us, event | category | flops | bytes accessed | tf_op | source)
XLA Modules:
  0.0 133.4 jit_solution(4059802011465897741)
XLA Ops:
  0.6 0.7 broadcast_in_dim.12
  1.3 27.2 %all_to_all.20 = bf16[16,8,180]{2,1,0:T(8,128)(2,1)S(1)} all-to-all(bf16[16,8,180]{2,1,0:T(8,128)(2,1)S(1)} %broadcast_in_dim.12), channel_id=1, replica_groups=mesh['zl'=4,'y'=4,'zh'=4,'x'=4,'core'=2] {'zl','zh'}, dimensions={0} | all-to-all | bytes 92160 | tf_op jit(solution)/shard_map/all_to_all | solution.py:211
  28.5 0.1 copy.18
  28.5 0.1 broadcast_in_dim.13
  28.6 0.1 broadcast_in_dim.14
  28.7 19.9 %all_to_all.21 = bf16[16,32,720]{2,1,0:T(8,128)(2,1)S(1)} all-to-all(bf16[16,32,720]{2,1,0:T(8,128)(2,1)S(1)} %broadcast_in_dim.14), channel_id=1, replica_groups=mesh['zl'=4,'y'=4,'zh'=4,'x'=4,'core'=2] {'y','x'}, dimensions={0} | all-to-all | bytes 1474560 | tf_op jit(solution)/shard_map/all_to_all | solution.py:211
  48.6 1.9 %collective-permute-start = (bf16[16,32,720]{2,1,0:T(8,128)(2,1)S(1)}, bf16[16,32,720]{2,1,0:T(8,128)(2,1)}, u32[]{:S(2)}, u32[]{:S(2)}) collective-permute-start(bf16[16,32,720]{2,1,0:T(8,128)(2,1)S(1)} %all_to_all.21), channel_id=1, source_target_pairs={{0,1},{1,0},{2,3},{3,2},{4,5},{5,4},{6,7},{7,6},{8,9},{9,8},{10,11... | collective-permute-start | bytes 2211848 | tf_op jit(solution)/shard_map/ppermute | solution.py:215
  50.6 0.2 fusion.1
  50.8 0.1 copy.21.sin_ref
  51.0 0.1 copy.20.cos_ref
  51.1 1.8 %collective-permute-done = bf16[16,32,720]{2,1,0:T(8,128)(2,1)} collective-permute-done((bf16[16,32,720]{2,1,0:T(8,128)(2,1)S(1)}, bf16[16,32,720]{2,1,0:T(8,128)(2,1)}, u32[]{:S(2)}, u32[]{:S(2)}) %collective-permute-start) | collective-permute-done | bytes 737312 | tf_op jit(solution)/shard_map/ppermute | solution.py:215
  52.9 1.2 broadcast_select_fusion.1
  54.1 0.2 maximum_bitcast_fusion
  54.3 0.0 copy-start
  54.3 0.0 copy-start.1
  54.3 0.2 copy.19
  54.5 1.1 copy-done
  55.6 0.0 copy-done.1
  55.6 0.0 copy-start.2
  55.6 1.7 %project.1 = (bf16[192,256]{1,0:T(8,128)(2,1)S(1)}, bf16[2,128,256]{2,1,0:T(8,128)(2,1)}) custom-call(bf16[192,2880]{1,0:T(8,128)(2,1)S(1)} %bitcast.26, bf16[4,256,720]{2,1,0:T(8,128)(2,1)S(1)} %bitcast.24, bf16[192,256]{1,0:T(8,128)(2,1)S(1)} %bitcast.28, f32[192,256]{1,0:T(8,128)S(1)} %copy.20.cos_ref, f32[192,256]{1,0:T(8,128)S(1)} %copy.21.sin_ref), custom_call_target="tpu_custom_call" | custom-call | tf_op jit(solution)/shard_map/project/pallas_call | solution.py:276
  57.2 2.7 %collective-permute-start.1 = (bf16[2,128,256]{2,1,0:T(8,128)(2,1)}, bf16[2,128,256]{2,1,0:T(8,128)(2,1)}, u32[]{:S(2)}, u32[]{:S(2)}) collective-permute-start(bf16[2,128,256]{2,1,0:T(8,128)(2,1)} %get-tuple-element.20), channel_id=1, source_target_pairs={{0,1},{1,2},{2,3},{3,4},{4,5},{5,6},{6,7},{7,8},{8,9},{9,10},{10,1... | collective-permute-start | bytes 393224 | tf_op jit(solution)/shard_map/ppermute | solution.py:286
  59.9 0.0 copy-done.2
  59.9 0.1 pad_dynamic-slice_fusion
  60.0 0.1 slice.39
  60.1 0.1 tile.35.qd_ref
  60.2 0.1 tile.37.qd_ref
  60.3 0.1 copy.23.kd_ref
  60.4 0.1 copy.22.kd_ref
  60.6 0.0 collective-permute-done.1.edge_ref
  60.6 6.1 %band_early.1 = (bf16[192,2048]{1,0:T(8,128)(2,1)}, f32[128,256]{1,0:T(8,128)S(1)}, f32[128,256]{1,0:T(8,128)S(1)}, bf16[2,128,256]{2,1,0:T(8,128)(2,1)S(1)}) custom-call(bf16[192,2048]{1,0:T(8,128)(2,1)} %bitcast.31, bf16[192,2048]{1,0:T(8,128)(2,1)} %bitcast.33, bf16[192,256]{1,0:T(8,128)(2,1)S(1)} %get-tuple-element.19.k_ref, ...), custom_call_target="tpu_custom_call" | custom-call | tf_op jit(solution)/shard_map/band_early/pallas_call | solution.py:312
  66.7 1.3 collective-permute-start.2
  68.0 0.1 fusion.order_ref
  68.1 4.1 %band_late.1 = (bf16[192,2048]{1,0:T(8,128)(2,1)}, f32[192,256]{1,0:T(8,128)S(1)}, f32[192,256]{1,0:T(8,128)S(1)}) custom-call(bf16[192,2048]{1,0:T(8,128)(2,1)} %bitcast.32, bf16[192,2048]{1,0:T(8,128)(2,1)} %bitcast.34, bf16[192,256]{1,0:T(8,128)(2,1)S(1)} %get-tuple-element.19.k_ref, ...), custom_call_target="tpu_custom_call", output_to_operand_aliasing={{0}: (6, {})} | custom-call | tf_op jit(solution)/shard_map/band_late/pallas_call | solution.py:338
  72.3 0.0 collective-permute-done.2.edge_ref
  72.3 1.6 %tail.1 = (bf16[192,256]{1,0:T(8,128)(2,1)}, bf16[192,256]{1,0:T(8,128)(2,1)S(1)}, f32[16,32,720]{2,1,0:T(8,128)S(1)}, bf16[16,32,720]{2,1,0:T(8,128)(2,1)S(1)}) custom-call(f32[128,256]{1,0:T(8,128)S(1)} %get-tuple-element.23.dk1_ref, f32[128,256]{1,0:T(8,128)S(1)} %get-tuple-element.24.dv1_ref, f32[192,256]{1,0:T(8,128)S(1)} %get-tuple-element.25.dk2_ref, ...), custom_call_target="tpu_custom_call" | custom-call | tf_op jit(solution)/shard_map/tail/pallas_call | solution.py:362
  73.9 4.8 %collective-permute-start.3 = (bf16[16,32,720]{2,1,0:T(8,128)(2,1)S(1)}, bf16[16,32,720]{2,1,0:T(8,128)(2,1)S(1)}, u32[]{:S(2)}, u32[]{:S(2)}) collective-permute-start(bf16[16,32,720]{2,1,0:T(8,128)(2,1)S(1)} %get-tuple-element.29), channel_id=1, source_target_pairs={{0,1},{1,0},{2,3},{3,2},{4,5},{5,4},{6,7},{7,6},{8,9},{9,8},{10,11... | collective-permute-start | bytes 2211848 | tf_op jit(solution)/shard_map/ppermute | solution.py:215
  78.7 1.8 %input_grad.1 = bf16[192,2880]{1,0:T(8,128)(2,1)} custom-call(bf16[192,256]{1,0:T(8,128)(2,1)S(1)} %get-tuple-element.30.lin_ref, bf16[4,256,720]{2,1,0:T(8,128)(2,1)S(1)} %bitcast.25), custom_call_target="tpu_custom_call" | custom-call | tf_op jit(solution)/shard_map/input_grad/pallas_call | solution.py:374
  80.5 0.1 collective-permute-done.3
  80.6 0.2 add_convert_fusion
  80.8 28.8 %all_to_all.22 = bf16[16,32,720]{2,1,0:T(8,128)(2,1)S(1)} all-to-all(bf16[16,32,720]{2,1,0:T(8,128)(2,1)S(1)} %add_convert_fusion), channel_id=1, replica_groups=mesh['zl'=4,'y'=4,'zh'=4,'x'=4,'core'=2] {'y','x'}, dimensions={0} | all-to-all | bytes 1474560 | tf_op jit(solution)/shard_map/all_to_all | solution.py:232
  109.6 0.1 reduce_sum.21
  109.8 0.1 reshape.159
  109.9 22.8 %all_to_all.23 = bf16[16,8,180]{2,1,0:T(8,128)(2,1)S(1)} all-to-all(bf16[16,8,180]{2,1,0:T(8,128)(2,1)S(1)} %bitcast.43), channel_id=1, replica_groups=mesh['zl'=4,'y'=4,'zh'=4,'x'=4,'core'=2] {'zl','zh'}, dimensions={0} | all-to-all | bytes 92160 | tf_op jit(solution)/shard_map/all_to_all | solution.py:232
  132.7 0.6 convert_reduce_fusion
  (13 shorter events, 0.1 us)
Async XLA Ops:
  48.6 4.3 %collective-permute-start = (bf16[16,32,720]{2,1,0:T(8,128)(2,1)S(1)}, bf16[16,32,720]{2,1,0:T(8,128)(2,1)}, u32[]{:S(2)}, u32[]{:S(2)}) collective-permute-start(bf16[16,32,720]{2,1,0:T(8,128)(2,1)S(1)} %all_to_all.21), channel_id=1, source_target_pairs={{0,1},{1,0},{2,3},{3,2},{4,5},{5,4},{6,7},{7,6},{8,9},{9,8},{10,11... | collective-permute-start | bytes 2211848 | tf_op jit(solution)/shard_map/ppermute | solution.py:215
  54.3 1.3 copy-start
  54.3 1.2 copy-start.1
  55.6 4.4 %copy-start.2 = (s32[1,6144]{1,0:T(1,128)S(1)}, s32[1,6144]{1,0:T(1,128)}, u32[]{:S(2)}) copy-start(s32[1,6144]{1,0:T(1,128)} %param.11) | copy-start | bytes 73732
  57.2 3.3 %collective-permute-start.1 = (bf16[2,128,256]{2,1,0:T(8,128)(2,1)}, bf16[2,128,256]{2,1,0:T(8,128)(2,1)}, u32[]{:S(2)}, u32[]{:S(2)}) collective-permute-start(bf16[2,128,256]{2,1,0:T(8,128)(2,1)} %get-tuple-element.20), channel_id=1, source_target_pairs={{0,1},{1,2},{2,3},{3,4},{4,5},{5,6},{6,7},{7,8},{8,9},{9,10},{10,1... | collective-permute-start | bytes 393224 | tf_op jit(solution)/shard_map/ppermute | solution.py:286
  66.7 5.5 %collective-permute-start.2 = (bf16[2,128,256]{2,1,0:T(8,128)(2,1)S(1)}, bf16[2,128,256]{2,1,0:T(8,128)(2,1)S(1)}, u32[]{:S(2)}, u32[]{:S(2)}) collective-permute-start(bf16[2,128,256]{2,1,0:T(8,128)(2,1)S(1)} %get-tuple-element.27), channel_id=1, source_target_pairs={{1,0},{2,1},{3,2},{4,3},{5,4},{6,5},{7,6},{8,7},{9,8},{10,9},{11,1... | collective-permute-start | bytes 393224 | tf_op jit(solution)/shard_map/ppermute | solution.py:336
  73.9 6.7 %collective-permute-start.3 = (bf16[16,32,720]{2,1,0:T(8,128)(2,1)S(1)}, bf16[16,32,720]{2,1,0:T(8,128)(2,1)S(1)}, u32[]{:S(2)}, u32[]{:S(2)}) collective-permute-start(bf16[16,32,720]{2,1,0:T(8,128)(2,1)S(1)} %get-tuple-element.29), channel_id=1, source_target_pairs={{0,1},{1,0},{2,3},{3,2},{4,5},{5,4},{6,7},{7,6},{8,9},{9,8},{10,11... | collective-permute-start | bytes 2211848 | tf_op jit(solution)/shard_map/ppermute | solution.py:215

commit v4 on v3

--- a/solution.py
+++ b/solution.py
@@ -51,19 +51,39 @@
             packed_ref[y, :, zl * width : (zl + 1) * width] = tokens_ref[:, at : at + width]
 
 
-def project_kernel(tokens_ref, weight_ref, v_ref, cos_ref, sin_ref, keys_ref, edge_ref, packed_ref):
-    parts, rows, _ = packed_ref.shape
+def half_linear(packed_ref, half_ref):
+    parts, rows, wide = packed_ref.shape
+    total = jnp.zeros((rows, KEYF // 2), f32)
+    for y in range(parts):
+        total += nt(packed_ref[y], half_ref[y * parts : (y + 1) * parts].reshape(KEYF // 2, wide))
+    return total
+
+
+def first_kernel(tokens_ref, mine_ref, packed_ref, linear_ref):
     pack(tokens_ref, packed_ref)
-    linear = jnp.zeros((rows, KEYF), f32)
-    for y in range(parts):
-        linear += nt(packed_ref[y], weight_ref[y])
-    keys = (linear * cos_ref[...] + swap_halves(linear) * sin_ref[...]).astype(bf16)
+    linear_ref[...] = half_linear(packed_ref, mine_ref)
+
+
+def table(ref):
+    return jnp.concatenate([ref[...], ref[...]], axis=1)
+
+
+def project_kernel(packed_ref, other_ref, linear_ref, order_ref, v_ref, cos_ref, sin_ref, keys_ref, edge_ref):
+    rows = packed_ref.shape[1]
+    gathered = jnp.concatenate([linear_ref[...], half_linear(packed_ref, other_ref)], axis=1)
+    top = gathered.astype(bf16)
+    rest = gathered - top.astype(f32)
+    middle = rest.astype(bf16)
+    bottom = (rest - middle.astype(f32)).astype(bf16)
+    order = order_ref[...]
+    linear = nn(top, order) + (nn(middle, order) + nn(bottom, order))
+    keys = (linear * table(cos_ref) + swap_halves(linear) * table(sin_ref)).astype(bf16)
     keys_ref[...] = keys
     edge_ref[0] = keys[rows - WINDOW :]
     edge_ref[1] = v_ref[rows - WINDOW :, :]
 
 
-def band_pairs(q_ref, g_ref, qd_ref, kd_ref, dq_ref, bias_ref, kk_ref, vv_ref, dka_ref, dva_ref, fill):
+def band_pairs(q_ref, g_ref, low_ref, dq_ref, bias_ref, kk_ref, vv_ref, dka_ref, dva_ref, fill):
     blocks = q_ref.shape[0] // ROWS
     span = ROWS + WINDOW
     lanes = GROUP * ROWS
@@ -71,12 +91,9 @@
     @pl.when(pl.program_id(0) == 0)
     def _():
         key_at = lax.broadcasted_iota(jnp.int32, (span, lanes), 0)
-        query_at = lax.broadcasted_iota(jnp.int32, (span, lanes), 1) % ROWS
-        distance = query_at + WINDOW - key_at
-        near = (distance >= 0) & (distance <= WINDOW)
+        last = lax.broadcasted_iota(jnp.int32, (1, lanes), 1) % ROWS + WINDOW
         for b in range(blocks):
-            same = kd_ref[b * ROWS : b * ROWS + span, :] == qd_ref[b]
-            bias_ref[b] = jnp.where(near & same, 0.0, masked_score)
+            bias_ref[b] = jnp.where((key_at >= low_ref[b]) & (key_at <= last), 0.0, masked_score)
 
     lane = lax.broadcasted_iota(jnp.int32, (ROWS, 2 * HEAD), 1)
     low = jnp.where(lane < HEAD, 1.0, 0.0).astype(bf16)
@@ -135,7 +152,7 @@
 
 
 def early_kernel(
-    q_ref, g_ref, k_ref, v_ref, edge_ref, qd_ref, kd_ref,
+    q_ref, g_ref, k_ref, v_ref, edge_ref, low_ref,
     dq_ref, dk_ref, dv_ref, out_edge_ref,
     bias_ref, kk_ref, vv_ref, dka_ref, dva_ref,
 ):
@@ -145,7 +162,7 @@
         vv_ref[:WINDOW, :] = doubled(edge_ref[1], head, 1.0)
         vv_ref[WINDOW:, :] = doubled(v_ref[...], head, 1.0)
 
-    dk, dv = band_pairs(q_ref, g_ref, qd_ref, kd_ref, dq_ref, bias_ref, kk_ref, vv_ref, dka_ref, dva_ref, fill)
+    dk, dv = band_pairs(q_ref, g_ref, low_ref, dq_ref, bias_ref, kk_ref, vv_ref, dka_ref, dva_ref, fill)
     out_edge_ref[0] = dk[:WINDOW].astype(bf16)
     out_edge_ref[1] = dv[:WINDOW].astype(bf16)
     dk_ref[...] = dk[WINDOW:]
@@ -153,7 +170,7 @@
 
 
 def late_kernel(
-    q_ref, g_ref, k_ref, v_ref, qd_ref, kd_ref, _,
+    q_ref, g_ref, k_ref, v_ref, low_ref, _,
     dq_ref, dk_ref, dv_ref,
     bias_ref, kk_ref, vv_ref, dka_ref, dva_ref,
 ):
@@ -161,7 +178,7 @@
         kk_ref[...] = doubled(k_ref[...], head, 0.125)
         vv_ref[...] = doubled(v_ref[...], head, 1.0)
 
-    dk, dv = band_pairs(q_ref, g_ref, qd_ref, kd_ref, dq_ref, bias_ref, kk_ref, vv_ref, dka_ref, dva_ref, fill)
+    dk, dv = band_pairs(q_ref, g_ref, low_ref, dq_ref, bias_ref, kk_ref, vv_ref, dka_ref, dva_ref, fill)
     dk_ref[...] = dk
     dv_ref[...] = dv
 
@@ -180,7 +197,7 @@
 
     vg_ref[...] = total(dv1_ref, dv2_ref, edge_ref[1]).astype(bf16)
     dk = total(dk1_ref, dk2_ref, edge_ref[0])
-    lin = (dk * cos_ref[...] - swap_halves(dk) * sin_ref[...]).astype(bf16)
+    lin = (dk * table(cos_ref) - swap_halves(dk) * table(sin_ref)).astype(bf16)
     lin_ref[...] = lin
     ordered = nt(order_ref[...], lin).astype(bf16)
     half = KEYF // 2
@@ -192,11 +209,16 @@
         send_ref[to] = nn(ordered[half:], packed_ref[y]).reshape(block).astype(bf16)
 
 
-def input_kernel(lin_ref, weight_ref, ig_ref):
-    parts = weight_ref.shape[0]
-    width = weight_ref.shape[2] // parts
+def input_kernel(lin_ref, order_ref, mine_ref, other_ref, ig_ref):
+    parts = 4
+    wide = mine_ref.shape[2]
+    width = wide // parts
+    half = KEYF // 2
+    ordered = nt(lin_ref[...], order_ref[...]).astype(bf16)
     for y in range(parts):
-        part = nn(lin_ref[...], weight_ref[y]).astype(bf16)
+        at = slice(y * parts, (y + 1) * parts)
+        part = nn(ordered[:, :half], mine_ref[at].reshape(half, wide))
+        part = (part + nn(ordered[:, half:], other_ref[at].reshape(half, wide))).astype(bf16)
         for zl in range(parts):
             at = (zl * parts + y) * width
             ig_ref[:, at : at + width] = part[:, zl * width : (zl + 1) * width]
@@ -217,15 +239,9 @@
 
 def gathered_weight(block):
     width, sub = block.shape
-    zl, y, zh, x = (lax.axis_size(a) for a in ("zl", "y", "zh", "x"))
+    zl, zh = lax.axis_size("zl"), lax.axis_size("zh")
     along_z = spread(block.T, Z).reshape(zl, zh, sub, width)
-    rows = along_z.transpose(1, 2, 0, 3).reshape(zh * sub, zl * width)
-    mine = spread(rows, YX)
-    other = exchanged(mine, "core")
-    first = lax.axis_index("core") == 0
-    pair = jnp.stack([jnp.where(first, mine, other), jnp.where(first, other, mine)])
-    pair = pair.reshape(2, y, x, zh, sub, zl * width).transpose(1, 3, 2, 0, 4, 5)
-    return pair.reshape(y, zh * x * 2 * sub, zl * width)
+    return spread(along_z.transpose(1, 2, 0, 3).reshape(zh * sub, zl * width), YX)
 
 
 def summed(x, axes):
@@ -251,35 +267,47 @@
     blocks = rows // ROWS
     parts = lax.axis_size("y")
     peers = lax.axis_size(CTX)
-    position = lax.axis_index(CTX)
+    mine = gathered_weight(key_weight)
+    mine, position, core, docs = lax.optimization_barrier(
+        (mine, lax.axis_index(CTX), lax.axis_index("core"), doc_ids[0])
+    )
     first_row = position * rows
 
-    exponent = jnp.arange(HEAD // 2, dtype=f32) * (-2.0 / HEAD)
+    lane = jnp.arange(2 * HEAD, dtype=jnp.int32)
+    exponent = (lane % (HEAD // 2)).astype(f32) * (-2.0 / HEAD)
     inverse_freq = jnp.power(f32(rope_base), exponent)
     angles = (first_row + jnp.arange(rows, dtype=jnp.int32)).astype(f32)[:, None] * inverse_freq[None, :]
-    cosine, sine = jnp.cos(angles), jnp.sin(angles)
-    cos_table = jnp.tile(cosine, (1, 2 * KV_HEADS))
-    sin_table = jnp.tile(jnp.concatenate([-sine, sine], axis=1), (1, KV_HEADS))
-
-    padded_docs = jnp.concatenate([jnp.full((WINDOW,), -1, jnp.int32), doc_ids[0]])
+    cos_table = jnp.cos(angles)
+    sin_table = jnp.sin(angles) * jnp.where(lane % HEAD < HEAD // 2, -1.0, 1.0)[None, :]
+
+    padded_docs = jnp.concatenate([jnp.full((WINDOW,), -1, jnp.int32), docs])
     band_docs = lax.dynamic_slice_in_dim(padded_docs, first_row, rows + WINDOW)
-    query_docs = jnp.tile(band_docs[WINDOW:].reshape(blocks, 1, ROWS), (1, 1, GROUP))
-    key_docs = band_docs[:, None]
-
-    core = lax.axis_index("core")
+    lowest = jnp.sum((band_docs[:, None] < band_docs[None, WINDOW:]).astype(jnp.int32), axis=0)
+    block_row = jnp.arange(rows, dtype=jnp.int32)
+    lowest = jnp.maximum(lowest - block_row // ROWS * ROWS, block_row % ROWS)
+    lowest = jnp.tile(lowest.reshape(blocks, 1, ROWS), (1, 1, GROUP))
+
     dest = jnp.arange(KEYF, dtype=jnp.int32)
     rel, dest_x, dest_zh, dest_j = dest // 128, dest // 32 % 4, dest // 8 % 4, dest % 8
     source = dest_zh * 64 + dest_x * 16 + (rel ^ core) * 8 + dest_j
     order = (source[:, None] == jnp.arange(KEYF, dtype=jnp.int32)[None, :]).astype(bf16)
 
-    weight = gathered_weight(key_weight)
+    other = exchanged(mine, "core")
+    packed, linear = pl.pallas_call(
+        first_kernel,
+        out_shape=[
+            jax.ShapeDtypeStruct((parts, rows, dim // parts), bf16),
+            jax.ShapeDtypeStruct((rows, KEYF // 2), f32),
+        ],
+        compiler_params=room(16),
+        name="project_own",
+    )(tokens, mine)
     keys, edge = pl.pallas_call(
         project_kernel,
         out_shape=[jax.ShapeDtypeStruct((rows, KEYF), bf16), jax.ShapeDtypeStruct((2, WINDOW, KEYF), bf16)],
-        scratch_shapes=[pltpu.VMEM((parts, rows, dim // parts), bf16)],
-        compiler_params=room(10),
+        compiler_params=room(16),
         name="project",
-    )(tokens, weight, v, cos_table, sin_table)
+    )(packed, other, linear, order, v, cos_table, sin_table)
 
     along = [(i, i + 1) for i in range(peers - 1)]
     back = [(i + 1, i) for i in range(peers - 1)]
@@ -295,9 +323,6 @@
 
     def heads(size, at):
         return pl.BlockSpec((size, wide), lambda k: (at, k))
-
-    def fixed(shape):
-        return pl.BlockSpec(shape, lambda k: (0,) * len(shape))
 
     def scratch(count):
         band = (count - 1) * ROWS + span
@@ -318,8 +343,7 @@
             tile(WINDOW),
             tile(WINDOW),
             edge_tile,
-            fixed((2, 1, GROUP * ROWS)),
-            fixed((2 * WINDOW, 1)),
+            pl.BlockSpec((2, 1, GROUP * ROWS), lambda k: (0, 0, 0)),
         ],
         out_specs=[heads(WINDOW, 0), tile(WINDOW), tile(WINDOW), edge_tile],
         out_shape=[
@@ -331,7 +355,7 @@
         scratch_shapes=scratch(2),
         compiler_params=room(16),
         name="band_early",
-    )(q, g, keys, v, prior, query_docs[:2], key_docs[: 2 * WINDOW])
+    )(q, g, keys, v, prior, lowest)
 
     incoming = lax.ppermute(out_edge, CTX, back)
 
@@ -343,8 +367,7 @@
             heads(ROWS, 2),
             tile(rows),
             tile(rows),
-            fixed((1, 1, GROUP * ROWS)),
-            fixed((rows, 1)),
+            pl.BlockSpec((1, 1, GROUP * ROWS), lambda k: (2, 0, 0)),
             pl.BlockSpec(memory_space=pl.ANY),
         ],
         out_specs=[heads(ROWS, 2), tile(rows), tile(rows)],
@@ -353,11 +376,11 @@
             jax.ShapeDtypeStruct((rows, KEYF), f32),
             jax.ShapeDtypeStruct((rows, KEYF), f32),
         ],
-        input_output_aliases={6: 0},
+        input_output_aliases={5: 0},
         scratch_shapes=scratch(1),
         compiler_params=room(16),
         name="band_late",
-    )(q, g, keys, v, query_docs[2:], key_docs[WINDOW:], dq)
+    )(q, g, keys, v, lowest, dq)
 
     value_grad, lin, own, send = pl.pallas_call(
         tail_kernel,
@@ -376,7 +399,7 @@
         out_shape=jax.ShapeDtypeStruct((rows, dim), bf16),
         compiler_params=room(8),
         name="input_grad",
-    )(lin, weight)
+    )(lin, order, mine, other)
 
     weight_grad, input_grad = scattered_gradient(own, send, input_grad, width, sub)
     return dq[None], value_grad[None], input_grad[None], weight_grad.T

time: 134 us -> 131 us (0.978)
  blocking collectives: 98.7 us -> 78.5 us
  waiting for transfers between devices: 1.98 us -> 14.5 us
  starting transfers between devices: 10.7 us -> 17.4 us
    all_to_all x2 -> x1, blocking collectives: 47 us -> 27.2 us  [spread(): lax.all_to_all(jnp.broadcast_to(x[None], (peers,) + x.shape), axes, 0, 0,...]
    all_to_all x0 -> x1, waiting for transfers between devices: none -> 13.1 us  [spread(): lax.all_to_all(jnp.broadcast_to(x[None], (peers,) + x.shape), axes, 0, 0,...]
    all_to_all x0 -> x1, starting transfers between devices: none -> 7.17 us  [spread(): lax.all_to_all(jnp.broadcast_to(x[None], (peers,) + x.shape), axes, 0, 0,...]
    ppermute x2, waiting for transfers between devices: 1.96 us -> 0.54 us  [exchanged(): return lax.ppermute(x, axis, [(0, 1), (1, 0)])]
  transfers between devices with their start and end apart: 4 -> 5, of which waited for: 2 -> 3; matrix products, arithmetic and copies ran while one was open for 1% -> 1% of each run, Pallas kernels for 4% -> 5%
where the time goes in v4:
time: 131 us
  blocking collectives  78.5 us (60%)
  starting transfers between devices  17.4 us (13%)
  Pallas kernels  15.6 us (12%)
  waiting for transfers between devices  14.5 us (11%)
  local copies, waits for them, and re-layouts  2.29 us (2%)
  other arithmetic  1.72 us (1%)
    all_to_all x2, blocking collectives, summed(): lax.all_to_all(x, axes, 0, 0, tiled=True).astype(f32)  51.4 us
    all_to_all x1, blocking collectives, spread(): lax.all_to_all(jnp.broadcast_to(x[None], (peers,) + x.shape), axes, 0, 0,...  27.2 us
    all_to_all x1, waiting for transfers between devices, spread(): lax.all_to_all(jnp.broadcast_to(x[None], (peers,) + x.shape), axes, 0, 0,...  13.1 us
    all_to_all x1, starting transfers between devices, spread(): lax.all_to_all(jnp.broadcast_to(x[None], (peers,) + x.shape), axes, 0, 0,...  7.17 us
    ppermute x2, starting transfers between devices, exchanged(): return lax.ppermute(x, axis, [(0, 1), (1, 0)])  6.92 us
    pallas_call x1, Pallas kernels, per_device(): pl.pallas_call(early_kernel, grid=(KV_HEADS // 2,), in_specs=[heads(WINDO...  5.99 us
    pallas_call x1, Pallas kernels, per_device(): pl.pallas_call(late_kernel, grid=(KV_HEADS // 2,), in_specs=[heads(ROWS,...  4.08 us
  transfers between devices with their start and end apart: 5, of which 3 were waited for; matrix products, arithmetic and copies ran while one was open for 1% of the time, Pallas kernels for 5%

profile of v4, /device:TPU:32, one launch (start us, length us, event | category | flops | bytes accessed | tf_op | source)
XLA Modules:
  0.0 130.8 jit_solution(10884929885305295852)
XLA Ops:
  0.6 0.0 copy-start.2
  0.6 0.0 copy-start
  0.7 0.8 broadcast_in_dim.20
  1.4 27.2 %all_to_all.20 = bf16[16,8,180]{2,1,0:T(8,128)(2,1)S(1)} all-to-all(bf16[16,8,180]{2,1,0:T(8,128)(2,1)S(1)} %broadcast_in_dim.20), channel_id=1, replica_groups=mesh['zl'=4,'y'=4,'zh'=4,'x'=4,'core'=2] {'zl','zh'}, dimensions={0} | all-to-all | bytes 92160 | tf_op jit(solution)/shard_map/all_to_all | solution.py:233
  28.6 0.1 copy.13
  28.6 0.1 broadcast_in_dim.21
  28.8 1.0 broadcast_in_dim.40
  29.7 0.0 copy-start.1
  29.7 7.2 %all-to-all-start.1 = ((bf16[16,32,720]{2,1,0:T(8,128)(2,1)}), bf16[16,32,720]{2,1,0:T(8,128)(2,1)S(1)}, u32[]{:S(2)}, u32[]{:S(2)}) async-start(bf16[16,32,720]{2,1,0:T(8,128)(2,1)} %broadcast_in_dim.40), calls=%async_computation.1 | async-start | bytes 1572864 | tf_op jit(solution)/shard_map/all_to_all | solution.py:233
  36.9 13.1 %all-to-all-done.1.mine_ref = bf16[16,32,720]{2,1,0:T(8,128)(2,1)S(1)} async-done(((bf16[16,32,720]{2,1,0:T(8,128)(2,1)}), bf16[16,32,720]{2,1,0:T(8,128)(2,1)S(1)}, u32[]{:S(2)}, u32[]{:S(2)}) %all-to-all-start.1) | async-done | bytes 737312 | tf_op jit(solution)/shard_map/all_to_all | solution.py:233
  50.0 0.0 copy-done.2
  50.0 0.1 pad_dynamic-slice_fusion
  50.1 1.9 %collective-permute-start = (bf16[16,32,720]{2,1,0:T(8,128)(2,1)S(1)}, bf16[16,32,720]{2,1,0:T(8,128)(2,1)S(1)}, u32[]{:S(2)}, u32[]{:S(2)}) collective-permute-start(bf16[16,32,720]{2,1,0:T(8,128)(2,1)S(1)} %all-to-all-done.1.mine_ref), channel_id=1, source_target_pairs={{0,1},{1,0},{2,3},{3,2},{4,5},{5,4},{6,7},{7,6},{8,9},{9,8},{10,11... | collective-permute-start | bytes 2211848 | tf_op jit(solution)/shard_map/ppermute | solution.py:237
  52.0 0.2 convert_reduce_fusion
  52.2 0.1 reduce_sum.33
  52.3 0.0 copy-done
  52.3 0.9 project_own.1
  53.2 0.1 fusion.order_ref
  53.3 0.4 fusion.1
  53.7 0.5 collective-permute-done.other_ref
  54.2 0.0 copy-done.1
  54.2 0.9 project.1
  55.1 2.1 %collective-permute-start.1 = (bf16[2,128,256]{2,1,0:T(8,128)(2,1)S(1)}, bf16[2,128,256]{2,1,0:T(8,128)(2,1)S(1)}, u32[]{:S(2)}, u32[]{:S(2)}) collective-permute-start(bf16[2,128,256]{2,1,0:T(8,128)(2,1)S(1)} %get-tuple-element.32), channel_id=1, source_target_pairs={{0,1},{1,2},{2,3},{3,4},{4,5},{5,6},{6,7},{7,8},{8,9},{9,10},{10,1... | collective-permute-start | bytes 393224 | tf_op jit(solution)/shard_map/ppermute | solution.py:314
  57.2 0.1 tile.9.low_ref
  57.3 0.8 collective-permute-done.1.edge_ref
  58.2 6.0 %band_early.1 = (bf16[192,2048]{1,0:T(8,128)(2,1)}, f32[128,256]{1,0:T(8,128)S(1)}, f32[128,256]{1,0:T(8,128)S(1)}, bf16[2,128,256]{2,1,0:T(8,128)(2,1)S(1)}) custom-call(bf16[192,2048]{1,0:T(8,128)(2,1)} %bitcast.20, bf16[192,2048]{1,0:T(8,128)(2,1)} %bitcast.22, bf16[192,256]{1,0:T(8,128)(2,1)S(1)} %get-tuple-element.30.k_ref, ...), custom_call_target="tpu_custom_call" | custom-call | tf_op jit(solution)/shard_map/band_early/pallas_call | solution.py:337
  64.2 1.3 collective-permute-start.2
  65.4 4.1 %band_late.1 = (bf16[192,2048]{1,0:T(8,128)(2,1)}, f32[192,256]{1,0:T(8,128)S(1)}, f32[192,256]{1,0:T(8,128)S(1)}) custom-call(bf16[192,2048]{1,0:T(8,128)(2,1)} %bitcast.21, bf16[192,2048]{1,0:T(8,128)(2,1)} %bitcast.23, bf16[192,256]{1,0:T(8,128)(2,1)S(1)} %get-tuple-element.30.k_ref, ...), custom_call_target="tpu_custom_call", output_to_operand_aliasing={{0}: (5, {})} | custom-call | tf_op jit(solution)/shard_map/band_late/pallas_call | solution.py:362
  69.5 0.0 collective-permute-done.2.edge_ref
  69.5 1.6 %tail.1 = (bf16[192,256]{1,0:T(8,128)(2,1)}, bf16[192,256]{1,0:T(8,128)(2,1)S(1)}, f32[16,32,720]{2,1,0:T(8,128)S(1)}, bf16[16,32,720]{2,1,0:T(8,128)(2,1)S(1)}) custom-call(f32[128,256]{1,0:T(8,128)S(1)} %get-tuple-element.35.dk1_ref, f32[128,256]{1,0:T(8,128)S(1)} %get-tuple-element.36.dv1_ref, f32[192,256]{1,0:T(8,128)S(1)} %get-tuple-element.37.dk2_ref, ...), custom_call_target="tpu_custom_call" | custom-call | tf_op jit(solution)/shard_map/tail/pallas_call | solution.py:385
  71.2 5.0 %collective-permute-start.3 = (bf16[16,32,720]{2,1,0:T(8,128)(2,1)S(1)}, bf16[16,32,720]{2,1,0:T(8,128)(2,1)S(1)}, u32[]{:S(2)}, u32[]{:S(2)}) collective-permute-start(bf16[16,32,720]{2,1,0:T(8,128)(2,1)S(1)} %get-tuple-element.41), channel_id=1, source_target_pairs={{0,1},{1,0},{2,3},{3,2},{4,5},{5,4},{6,7},{7,6},{8,9},{9,8},{10,11... | collective-permute-start | bytes 2211848 | tf_op jit(solution)/shard_map/ppermute | solution.py:237
  76.2 2.1 %input_grad.1 = bf16[192,2880]{1,0:T(8,128)(2,1)} custom-call(bf16[192,256]{1,0:T(8,128)(2,1)S(1)} %get-tuple-element.42.lin_ref, bf16[256,256]{1,0:T(8,128)(2,1)S(1)} %fusion.order_ref, bf16[16,32,720]{2,1,0:T(8,128)(2,1)S(1)} %all-to-all-done.1.mine_ref, bf16[16,32,720]{2,1,0:T(8,128)(2,1)S(1)} %collective-permute-done.other_ref), custom_call_target="tpu_custom_call" | custom-call | tf_op jit(solution)/shard_map/input_grad/pallas_call | solution.py:397
  78.3 0.0 collective-permute-done.3
  78.3 0.2 add_convert_fusion
  78.5 28.6 %all_to_all.21 = bf16[16,32,720]{2,1,0:T(8,128)(2,1)S(1)} all-to-all(bf16[16,32,720]{2,1,0:T(8,128)(2,1)S(1)} %add_convert_fusion), channel_id=1, replica_groups=mesh['zl'=4,'y'=4,'zh'=4,'x'=4,'core'=2] {'y','x'}, dimensions={0} | all-to-all | bytes 1474560 | tf_op jit(solution)/shard_map/all_to_all | solution.py:248
  107.1 0.1 reduce_sum.34
  107.2 0.1 reshape.167
  107.3 22.8 %all_to_all.22 = bf16[16,8,180]{2,1,0:T(8,128)(2,1)S(1)} all-to-all(bf16[16,8,180]{2,1,0:T(8,128)(2,1)S(1)} %bitcast.28), channel_id=1, replica_groups=mesh['zl'=4,'y'=4,'zh'=4,'x'=4,'core'=2] {'zl','zh'}, dimensions={0} | all-to-all | bytes 92160 | tf_op jit(solution)/shard_map/all_to_all | solution.py:248
  130.2 0.6 convert_reduce_fusion.1
  (7 shorter events, 0.1 us)
Async XLA Ops:
  0.6 49.4 %copy-start.2 = (s32[1,6144]{1,0:T(1,128)S(1)}, s32[1,6144]{1,0:T(1,128)}, u32[]{:S(2)}) copy-start(s32[1,6144]{1,0:T(1,128)} %param.11) | copy-start | bytes 73732
  0.6 51.6 %copy-start = (bf16[1,192,2880]{2,1,0:T(8,128)(2,1)S(1)}, bf16[1,192,2880]{2,1,0:T(8,128)(2,1)}, u32[]{:S(2)}) copy-start(bf16[1,192,2880]{2,1,0:T(8,128)(2,1)} %param.6) | copy-start | bytes 3317764
  29.7 24.5 %copy-start.1 = (bf16[1,192,256]{2,1,0:T(8,128)(2,1)S(1)}, bf16[1,192,256]{2,1,0:T(8,128)(2,1)}, u32[]{:S(2)}) copy-start(bf16[1,192,256]{2,1,0:T(8,128)(2,1)} %param.8) | copy-start | bytes 294916
  29.7 20.3 %all-to-all-start.1 = ((bf16[16,32,720]{2,1,0:T(8,128)(2,1)}), bf16[16,32,720]{2,1,0:T(8,128)(2,1)S(1)}, u32[]{:S(2)}, u32[]{:S(2)}) async-start(bf16[16,32,720]{2,1,0:T(8,128)(2,1)} %broadcast_in_dim.40), calls=%async_computation.1 | async-start | bytes 1572864 | tf_op jit(solution)/shard_map/all_to_all | solution.py:233
  50.1 4.2 %collective-permute-start = (bf16[16,32,720]{2,1,0:T(8,128)(2,1)S(1)}, bf16[16,32,720]{2,1,0:T(8,128)(2,1)S(1)}, u32[]{:S(2)}, u32[]{:S(2)}) collective-permute-start(bf16[16,32,720]{2,1,0:T(8,128)(2,1)S(1)} %all-to-all-done.1.mine_ref), channel_id=1, source_target_pairs={{0,1},{1,0},{2,3},{3,2},{4,5},{5,4},{6,7},{7,6},{8,9},{9,8},{10,11... | collective-permute-start | bytes 2211848 | tf_op jit(solution)/shard_map/ppermute | solution.py:237
  55.1 3.0 %collective-permute-start.1 = (bf16[2,128,256]{2,1,0:T(8,128)(2,1)S(1)}, bf16[2,128,256]{2,1,0:T(8,128)(2,1)S(1)}, u32[]{:S(2)}, u32[]{:S(2)}) collective-permute-start(bf16[2,128,256]{2,1,0:T(8,128)(2,1)S(1)} %get-tuple-element.32), channel_id=1, source_target_pairs={{0,1},{1,2},{2,3},{3,4},{4,5},{5,6},{6,7},{7,8},{8,9},{9,10},{10,1... | collective-permute-start | bytes 393224 | tf_op jit(solution)/shard_map/ppermute | solution.py:314
  64.2 5.4 %collective-permute-start.2 = (bf16[2,128,256]{2,1,0:T(8,128)(2,1)S(1)}, bf16[2,128,256]{2,1,0:T(8,128)(2,1)S(1)}, u32[]{:S(2)}, u32[]{:S(2)}) collective-permute-start(bf16[2,128,256]{2,1,0:T(8,128)(2,1)S(1)} %get-tuple-element.39), channel_id=1, source_target_pairs={{1,0},{2,1},{3,2},{4,3},{5,4},{6,5},{7,6},{8,7},{9,8},{10,9},{11,1... | collective-permute-start | bytes 393224 | tf_op jit(solution)/shard_map/ppermute | solution.py:360
  71.2 7.1 %collective-permute-start.3 = (bf16[16,32,720]{2,1,0:T(8,128)(2,1)S(1)}, bf16[16,32,720]{2,1,0:T(8,128)(2,1)S(1)}, u32[]{:S(2)}, u32[]{:S(2)}) collective-permute-start(bf16[16,32,720]{2,1,0:T(8,128)(2,1)S(1)} %get-tuple-element.41), channel_id=1, source_target_pairs={{0,1},{1,0},{2,3},{3,2},{4,5},{5,4},{6,7},{7,6},{8,9},{9,8},{10,11... | collective-permute-start | bytes 2211848 | tf_op jit(solution)/shard_map/ppermute | solution.py:237

commit v5 on v4

--- a/solution.py
+++ b/solution.py
@@ -68,7 +68,7 @@
     return jnp.concatenate([ref[...], ref[...]], axis=1)
 
 
-def project_kernel(packed_ref, other_ref, linear_ref, order_ref, v_ref, cos_ref, sin_ref, keys_ref, edge_ref):
+def project_kernel(packed_ref, other_ref, linear_ref, order_ref, cos_ref, sin_ref, keys_ref, edge_ref):
     rows = packed_ref.shape[1]
     gathered = jnp.concatenate([linear_ref[...], half_linear(packed_ref, other_ref)], axis=1)
     top = gathered.astype(bf16)
@@ -79,8 +79,7 @@
     linear = nn(top, order) + (nn(middle, order) + nn(bottom, order))
     keys = (linear * table(cos_ref) + swap_halves(linear) * table(sin_ref)).astype(bf16)
     keys_ref[...] = keys
-    edge_ref[0] = keys[rows - WINDOW :]
-    edge_ref[1] = v_ref[rows - WINDOW :, :]
+    edge_ref[...] = keys[rows - WINDOW :]
 
 
 def band_pairs(q_ref, g_ref, low_ref, dq_ref, bias_ref, kk_ref, vv_ref, dka_ref, dva_ref, fill):
@@ -152,14 +151,14 @@
 
 
 def early_kernel(
-    q_ref, g_ref, k_ref, v_ref, edge_ref, low_ref,
+    q_ref, g_ref, k_ref, v_ref, prior_k_ref, prior_v_ref, low_ref,
     dq_ref, dk_ref, dv_ref, out_edge_ref,
     bias_ref, kk_ref, vv_ref, dka_ref, dva_ref,
 ):
     def fill(head):
-        kk_ref[:WINDOW, :] = doubled(edge_ref[0], head, 0.125)
+        kk_ref[:WINDOW, :] = doubled(prior_k_ref[...], head, 0.125)
         kk_ref[WINDOW:, :] = doubled(k_ref[...], head, 0.125)
-        vv_ref[:WINDOW, :] = doubled(edge_ref[1], head, 1.0)
+        vv_ref[:WINDOW, :] = doubled(prior_v_ref[...], head, 1.0)
         vv_ref[WINDOW:, :] = doubled(v_ref[...], head, 1.0)
 
     dk, dv = band_pairs(q_ref, g_ref, low_ref, dq_ref, bias_ref, kk_ref, vv_ref, dka_ref, dva_ref, fill)
@@ -183,20 +182,19 @@
     dv_ref[...] = dv
 
 
+def total(early_ref, late_ref, edge):
+    sums = late_ref[...]
+    start = sums.shape[0] - WINDOW
+    sums = jnp.concatenate([sums[:WINDOW] + early_ref[...], sums[WINDOW:]], axis=0)
+    return jnp.concatenate([sums[:start], sums[start:] + edge.astype(f32)], axis=0)
+
+
 def tail_kernel(
-    dk1_ref, dv1_ref, dk2_ref, dv2_ref, edge_ref, cos_ref, sin_ref, tokens_ref, order_ref,
-    vg_ref, lin_ref, own_ref, send_ref, packed_ref,
+    early_ref, late_ref, edge_ref, cos_ref, sin_ref, tokens_ref, order_ref,
+    lin_ref, own_ref, send_ref, packed_ref,
 ):
     parts, rows, wide = packed_ref.shape
-    start = rows - WINDOW
-
-    def total(early_ref, late_ref, edge):
-        sums = late_ref[...]
-        sums = jnp.concatenate([sums[:WINDOW] + early_ref[...], sums[WINDOW:]], axis=0)
-        return jnp.concatenate([sums[:start], sums[start:] + edge.astype(f32)], axis=0)
-
-    vg_ref[...] = total(dv1_ref, dv2_ref, edge_ref[1]).astype(bf16)
-    dk = total(dk1_ref, dk2_ref, edge_ref[0])
+    dk = total(early_ref, late_ref, edge_ref[0])
     lin = (dk * table(cos_ref) - swap_halves(dk) * table(sin_ref)).astype(bf16)
     lin_ref[...] = lin
     ordered = nt(order_ref[...], lin).astype(bf16)
@@ -209,7 +207,8 @@
         send_ref[to] = nn(ordered[half:], packed_ref[y]).reshape(block).astype(bf16)
 
 
-def input_kernel(lin_ref, order_ref, mine_ref, other_ref, ig_ref):
+def input_kernel(lin_ref, order_ref, mine_ref, other_ref, early_ref, late_ref, edge_ref, ig_ref, vg_ref):
+    vg_ref[...] = total(early_ref, late_ref, edge_ref[1]).astype(bf16)
     parts = 4
     wide = mine_ref.shape[2]
     width = wide // parts
@@ -267,6 +266,10 @@
     blocks = rows // ROWS
     parts = lax.axis_size("y")
     peers = lax.axis_size(CTX)
+    along = [(i, i + 1) for i in range(peers - 1)]
+    back = [(i + 1, i) for i in range(peers - 1)]
+    prior_v = lax.ppermute(v[rows - WINDOW :], CTX, along)
+
     mine = gathered_weight(key_weight)
     mine, position, core, docs = lax.optimization_barrier(
         (mine, lax.axis_index(CTX), lax.axis_index("core"), doc_ids[0])
@@ -304,19 +307,16 @@
     )(tokens, mine)
     keys, edge = pl.pallas_call(
         project_kernel,
-        out_shape=[jax.ShapeDtypeStruct((rows, KEYF), bf16), jax.ShapeDtypeStruct((2, WINDOW, KEYF), bf16)],
+        out_shape=[jax.ShapeDtypeStruct((rows, KEYF), bf16), jax.ShapeDtypeStruct((WINDOW, KEYF), bf16)],
         compiler_params=room(16),
         name="project",
-    )(packed, other, linear, order, v, cos_table, sin_table)
-
-    along = [(i, i + 1) for i in range(peers - 1)]
-    back = [(i + 1, i) for i in range(peers - 1)]
-    prior = lax.ppermute(edge, CTX, along)
+    )(packed, other, linear, order, cos_table, sin_table)
+
+    prior_k = lax.ppermute(edge, CTX, along)
 
     span = ROWS + WINDOW
     pair = 2 * HEAD
     wide = 2 * GROUP * HEAD
-    edge_tile = pl.BlockSpec((2, WINDOW, pair), lambda k: (0, 0, k))
 
     def tile(size):
         return pl.BlockSpec((size, pair), lambda k: (0, k))
@@ -342,10 +342,11 @@
             heads(WINDOW, 0),
             tile(WINDOW),
             tile(WINDOW),
-            edge_tile,
+            tile(WINDOW),
+            tile(WINDOW),
             pl.BlockSpec((2, 1, GROUP * ROWS), lambda k: (0, 0, 0)),
         ],
-        out_specs=[heads(WINDOW, 0), tile(WINDOW), tile(WINDOW), edge_tile],
+        out_specs=[heads(WINDOW, 0), tile(WINDOW), tile(WINDOW), pl.BlockSpec((2, WINDOW, pair), lambda k: (0, 0, k))],
         out_shape=[
             jax.ShapeDtypeStruct((rows, QUERY_HEADS * HEAD), bf16),
             jax.ShapeDtypeStruct((WINDOW, KEYF), f32),
@@ -355,7 +356,7 @@
         scratch_shapes=scratch(2),
         compiler_params=room(16),
         name="band_early",
-    )(q, g, keys, v, prior, lowest)
+    )(q, g, keys, v, prior_k, prior_v, lowest)
 
     incoming = lax.ppermute(out_edge, CTX, back)
 
@@ -382,26 +383,25 @@
         name="band_late",
     )(q, g, keys, v, lowest, dq)
 
-    value_grad, lin, own, send = pl.pallas_call(
+    lin, own, send = pl.pallas_call(
         tail_kernel,
         out_shape=[
             jax.ShapeDtypeStruct((rows, KEYF), bf16),
-            jax.ShapeDtypeStruct((rows, KEYF), bf16),
             jax.ShapeDtypeStruct((parts * parts, KEYF // 2 // parts, dim // parts), f32),
             jax.ShapeDtypeStruct((parts * parts, KEYF // 2 // parts, dim // parts), bf16),
         ],
         scratch_shapes=[pltpu.VMEM((parts, rows, dim // parts), bf16)],
         compiler_params=room(16),
         name="tail",
-    )(dk1, dv1, dk2, dv2, incoming, cos_table, sin_table, tokens, order)
-    input_grad = pl.pallas_call(
+    )(dk1, dk2, incoming, cos_table, sin_table, tokens, order)
+    beside = pl.pallas_call(
         input_kernel,
-        out_shape=jax.ShapeDtypeStruct((rows, dim), bf16),
+        out_shape=[jax.ShapeDtypeStruct((rows, dim), bf16), jax.ShapeDtypeStruct((rows, KEYF), bf16)],
         compiler_params=room(8),
         name="input_grad",
-    )(lin, order, mine, other)
-
-    weight_grad, input_grad = scattered_gradient(own, send, input_grad, width, sub)
+    )(lin, order, mine, other, dv1, dv2, incoming)
+
+    weight_grad, (input_grad, value_grad) = scattered_gradient(own, send, beside, width, sub)
     return dq[None], value_grad[None], input_grad[None], weight_grad.T
 
 

time: 131 us -> 129 us (0.985)
    ppermute x1 -> x2, starting transfers between devices: 2.05 us -> 3.34 us  [the longest x1 2.04 us: per_device(): prior_k = lax.ppermute(edge, CTX, along)]
  transfers between devices with their start and end apart: 5 -> 6, of which waited for: 3 -> 3; matrix products, arithmetic and copies ran while one was open for 1% -> 1% of each run, Pallas kernels for 5% -> 6%
where the time goes in v5:
time: 129 us
  blocking collectives  78.1 us (61%)
  starting transfers between devices  17.4 us (13%)
  Pallas kernels  15 us (12%)
  waiting for transfers between devices  13.7 us (11%)
  local copies, waits for them, and re-layouts  2.3 us (2%)
  other arithmetic  1.68 us (1%)
    all_to_all x2, blocking collectives, summed(): lax.all_to_all(x, axes, 0, 0, tiled=True).astype(f32)  50.9 us
    all_to_all x1, blocking collectives, spread(): lax.all_to_all(jnp.broadcast_to(x[None], (peers,) + x.shape), axes, 0, 0,...  27.2 us
    all_to_all x1, waiting for transfers between devices, spread(): lax.all_to_all(jnp.broadcast_to(x[None], (peers,) + x.shape), axes, 0, 0,...  12.4 us
    all_to_all x1, starting transfers between devices, spread(): lax.all_to_all(jnp.broadcast_to(x[None], (peers,) + x.shape), axes, 0, 0,...  7.03 us
    pallas_call x1, Pallas kernels, per_device(): pl.pallas_call(early_kernel, grid=(KV_HEADS // 2,), in_specs=[heads(WINDO...  5.99 us
    ppermute x2, starting transfers between devices, exchanged(): return lax.ppermute(x, axis, [(0, 1), (1, 0)])  5.78 us
    pallas_call x1, Pallas kernels, per_device(): pl.pallas_call(late_kernel, grid=(KV_HEADS // 2,), in_specs=[heads(ROWS,...  4.08 us
  transfers between devices with their start and end apart: 6, of which 3 were waited for; matrix products, arithmetic and copies ran while one was open for 1% of the time, Pallas kernels for 6%

profile of v5, /device:TPU:32, one launch (start us, length us, event | category | flops | bytes accessed | tf_op | source)
XLA Modules:
  0.0 129.0 jit_solution(14955300610941522343)
XLA Ops:
  0.6 0.0 copy-start.1
  0.6 0.0 copy-start.2
  0.7 0.0 copy-start
  0.7 0.8 broadcast_in_dim.20
  1.4 27.2 %all_to_all.20 = bf16[16,8,180]{2,1,0:T(8,128)(2,1)S(1)} all-to-all(bf16[16,8,180]{2,1,0:T(8,128)(2,1)S(1)} %broadcast_in_dim.20), channel_id=1, replica_groups=mesh['zl'=4,'y'=4,'zh'=4,'x'=4,'core'=2] {'zl','zh'}, dimensions={0} | all-to-all | bytes 92160 | tf_op jit(solution)/shard_map/all_to_all | solution.py:232
  28.6 0.1 copy.13
  28.7 0.1 broadcast_in_dim.21
  28.8 1.0 broadcast_in_dim.40
  29.7 7.0 %all-to-all-start.1 = ((bf16[16,32,720]{2,1,0:T(8,128)(2,1)}), bf16[16,32,720]{2,1,0:T(8,128)(2,1)S(1)}, u32[]{:S(2)}, u32[]{:S(2)}) async-start(bf16[16,32,720]{2,1,0:T(8,128)(2,1)} %broadcast_in_dim.40), calls=%async_computation.1 | async-start | bytes 1572864 | tf_op jit(solution)/shard_map/all_to_all | solution.py:232
  36.8 0.0 copy-done.1
  36.8 1.3 %collective-permute-start.2 = (bf16[128,256]{1,0:T(8,128)(2,1)S(1)}, bf16[128,256]{1,0:T(8,128)(2,1)S(1)}, u32[]{:S(2)}, u32[]{:S(2)}) collective-permute-start(bf16[128,256]{1,0:T(8,128)(2,1)S(1)} %slice_bitcast_fusion), channel_id=1, source_target_pairs={{0,1},{1,2},{2,3},{3,4},{4,5},{5,6},{6,7},{7,8},{8,9},{9,10},{10,1... | collective-permute-start | bytes 196616 | tf_op jit(solution)/shard_map/ppermute | solution.py:271
  38.1 12.4 %all-to-all-done.1.mine_ref = bf16[16,32,720]{2,1,0:T(8,128)(2,1)S(1)} async-done(((bf16[16,32,720]{2,1,0:T(8,128)(2,1)}), bf16[16,32,720]{2,1,0:T(8,128)(2,1)S(1)}, u32[]{:S(2)}, u32[]{:S(2)}) %all-to-all-start.1) | async-done | bytes 737312 | tf_op jit(solution)/shard_map/all_to_all | solution.py:232
  50.5 0.0 copy-done.2
  50.5 0.1 pad_dynamic-slice_fusion
  50.6 1.9 %collective-permute-start = (bf16[16,32,720]{2,1,0:T(8,128)(2,1)S(1)}, bf16[16,32,720]{2,1,0:T(8,128)(2,1)S(1)}, u32[]{:S(2)}, u32[]{:S(2)}) collective-permute-start(bf16[16,32,720]{2,1,0:T(8,128)(2,1)S(1)} %all-to-all-done.1.mine_ref), channel_id=1, source_target_pairs={{0,1},{1,0},{2,3},{3,2},{4,5},{5,4},{6,7},{7,6},{8,9},{9,8},{10,11... | collective-permute-start | bytes 2211848 | tf_op jit(solution)/shard_map/ppermute | solution.py:236
  52.5 0.2 convert_reduce_fusion
  52.7 0.1 reduce_sum.33
  52.8 0.0 copy-done
  52.8 0.9 project_own.1
  53.7 0.1 fusion.order_ref
  53.8 0.4 fusion.1
  54.2 0.5 collective-permute-done.other_ref
  54.8 0.9 project.1
  55.7 2.0 %collective-permute-start.1 = (bf16[128,256]{1,0:T(8,128)(2,1)S(1)}, bf16[128,256]{1,0:T(8,128)(2,1)S(1)}, u32[]{:S(2)}, u32[]{:S(2)}) collective-permute-start(bf16[128,256]{1,0:T(8,128)(2,1)S(1)} %get-tuple-element.34), channel_id=1, source_target_pairs={{0,1},{1,2},{2,3},{3,4},{4,5},{5,6},{6,7},{7,8},{8,9},{9,10},{10,1... | collective-permute-start | bytes 196616 | tf_op jit(solution)/shard_map/ppermute | solution.py:315
  57.8 0.1 tile.9.low_ref
  57.8 0.0 collective-permute-done.2.prior_v_ref
  57.9 0.8 collective-permute-done.1.prior_k_ref
  58.6 6.0 %band_early.1 = (bf16[192,2048]{1,0:T(8,128)(2,1)}, f32[128,256]{1,0:T(8,128)S(1)}, f32[128,256]{1,0:T(8,128)S(1)}, bf16[2,128,256]{2,1,0:T(8,128)(2,1)S(1)}) custom-call(bf16[192,2048]{1,0:T(8,128)(2,1)} %bitcast.21, bf16[192,2048]{1,0:T(8,128)(2,1)} %bitcast.23, bf16[192,256]{1,0:T(8,128)(2,1)S(1)} %get-tuple-element.32.k_ref, ...), custom_call_target="tpu_custom_call" | custom-call | tf_op jit(solution)/shard_map/band_early/pallas_call | solution.py:337
  64.6 1.3 collective-permute-start.3
  65.9 4.1 %band_late.1 = (bf16[192,2048]{1,0:T(8,128)(2,1)}, f32[192,256]{1,0:T(8,128)S(1)}, f32[192,256]{1,0:T(8,128)S(1)}) custom-call(bf16[192,2048]{1,0:T(8,128)(2,1)} %bitcast.22, bf16[192,2048]{1,0:T(8,128)(2,1)} %bitcast.24, bf16[192,256]{1,0:T(8,128)(2,1)S(1)} %get-tuple-element.32.k_ref, ...), custom_call_target="tpu_custom_call", output_to_operand_aliasing={{0}: (5, {})} | custom-call | tf_op jit(solution)/shard_map/band_late/pallas_call | solution.py:363
  70.0 0.0 collective-permute-done.3.edge_ref
  70.0 1.0 tail.1
  71.0 3.9 %collective-permute-start.4 = (bf16[16,32,720]{2,1,0:T(8,128)(2,1)S(1)}, bf16[16,32,720]{2,1,0:T(8,128)(2,1)S(1)}, u32[]{:S(2)}, u32[]{:S(2)}) collective-permute-start(bf16[16,32,720]{2,1,0:T(8,128)(2,1)S(1)} %get-tuple-element.40), channel_id=1, source_target_pairs={{0,1},{1,0},{2,3},{3,2},{4,5},{5,4},{6,7},{7,6},{8,9},{9,8},{10,11... | collective-permute-start | bytes 2211848 | tf_op jit(solution)/shard_map/ppermute | solution.py:236
  74.9 2.1 %input_grad.1 = (bf16[192,2880]{1,0:T(8,128)(2,1)}, bf16[192,256]{1,0:T(8,128)(2,1)}) custom-call(bf16[192,256]{1,0:T(8,128)(2,1)S(1)} %get-tuple-element.41.lin_ref, bf16[256,256]{1,0:T(8,128)(2,1)S(1)} %fusion.order_ref, bf16[16,32,720]{2,1,0:T(8,128)(2,1)S(1)} %all-to-all-done.1.mine_ref, bf16[16,32,720]{2,1,0:T(8,128)(2,1)S(1)} %collective-permute-done.other_ref, ...), custom_call_target="tpu_custom_call" | custom-call | tf_op jit(solution)/shard_map/input_grad/pallas_call | solution.py:397
  77.0 0.0 collective-permute-done.4
  77.0 0.2 add_convert_fusion
  77.2 28.7 %all_to_all.21 = bf16[16,32,720]{2,1,0:T(8,128)(2,1)S(1)} all-to-all(bf16[16,32,720]{2,1,0:T(8,128)(2,1)S(1)} %add_convert_fusion), channel_id=1, replica_groups=mesh['zl'=4,'y'=4,'zh'=4,'x'=4,'core'=2] {'y','x'}, dimensions={0} | all-to-all | bytes 1474560 | tf_op jit(solution)/shard_map/all_to_all | solution.py:247
  105.9 0.1 reduce_sum.34
  106.0 0.1 reshape.168
  106.2 22.2 %all_to_all.22 = bf16[16,8,180]{2,1,0:T(8,128)(2,1)S(1)} all-to-all(bf16[16,8,180]{2,1,0:T(8,128)(2,1)S(1)} %bitcast.28), channel_id=1, replica_groups=mesh['zl'=4,'y'=4,'zh'=4,'x'=4,'core'=2] {'zl','zh'}, dimensions={0} | all-to-all | bytes 92160 | tf_op jit(solution)/shard_map/all_to_all | solution.py:247
  128.4 0.6 convert_reduce_fusion.1
  (8 shorter events, 0.1 us)
Async XLA Ops:
  0.6 36.1 %copy-start.1 = (bf16[1,192,256]{2,1,0:T(8,128)(2,1)S(1)}, bf16[1,192,256]{2,1,0:T(8,128)(2,1)}, u32[]{:S(2)}) copy-start(bf16[1,192,256]{2,1,0:T(8,128)(2,1)} %param.8) | copy-start | bytes 294916
  0.6 49.9 %copy-start.2 = (s32[1,6144]{1,0:T(1,128)S(1)}, s32[1,6144]{1,0:T(1,128)}, u32[]{:S(2)}) copy-start(s32[1,6144]{1,0:T(1,128)} %param.11) | copy-start | bytes 73732
  0.7 52.2 %copy-start = (bf16[1,192,2880]{2,1,0:T(8,128)(2,1)S(1)}, bf16[1,192,2880]{2,1,0:T(8,128)(2,1)}, u32[]{:S(2)}) copy-start(bf16[1,192,2880]{2,1,0:T(8,128)(2,1)} %param.6) | copy-start | bytes 3317764
  29.7 20.8 %all-to-all-start.1 = ((bf16[16,32,720]{2,1,0:T(8,128)(2,1)}), bf16[16,32,720]{2,1,0:T(8,128)(2,1)S(1)}, u32[]{:S(2)}, u32[]{:S(2)}) async-start(bf16[16,32,720]{2,1,0:T(8,128)(2,1)} %broadcast_in_dim.40), calls=%async_computation.1 | async-start | bytes 1572864 | tf_op jit(solution)/shard_map/all_to_all | solution.py:232
  36.8 21.1 %collective-permute-start.2 = (bf16[128,256]{1,0:T(8,128)(2,1)S(1)}, bf16[128,256]{1,0:T(8,128)(2,1)S(1)}, u32[]{:S(2)}, u32[]{:S(2)}) collective-permute-start(bf16[128,256]{1,0:T(8,128)(2,1)S(1)} %slice_bitcast_fusion), channel_id=1, source_target_pairs={{0,1},{1,2},{2,3},{3,4},{4,5},{5,6},{6,7},{7,8},{8,9},{9,10},{10,1... | collective-permute-start | bytes 196616 | tf_op jit(solution)/shard_map/ppermute | solution.py:271
  50.6 4.2 %collective-permute-start = (bf16[16,32,720]{2,1,0:T(8,128)(2,1)S(1)}, bf16[16,32,720]{2,1,0:T(8,128)(2,1)S(1)}, u32[]{:S(2)}, u32[]{:S(2)}) collective-permute-start(bf16[16,32,720]{2,1,0:T(8,128)(2,1)S(1)} %all-to-all-done.1.mine_ref), channel_id=1, source_target_pairs={{0,1},{1,0},{2,3},{3,2},{4,5},{5,4},{6,7},{7,6},{8,9},{9,8},{10,11... | collective-permute-start | bytes 2211848 | tf_op jit(solution)/shard_map/ppermute | solution.py:236
  55.7 2.9 %collective-permute-start.1 = (bf16[128,256]{1,0:T(8,128)(2,1)S(1)}, bf16[128,256]{1,0:T(8,128)(2,1)S(1)}, u32[]{:S(2)}, u32[]{:S(2)}) collective-permute-start(bf16[128,256]{1,0:T(8,128)(2,1)S(1)} %get-tuple-element.34), channel_id=1, source_target_pairs={{0,1},{1,2},{2,3},{3,4},{4,5},{5,6},{6,7},{7,8},{8,9},{9,10},{10,1... | collective-permute-start | bytes 196616 | tf_op jit(solution)/shard_map/ppermute | solution.py:315
  64.6 5.4 %collective-permute-start.3 = (bf16[2,128,256]{2,1,0:T(8,128)(2,1)S(1)}, bf16[2,128,256]{2,1,0:T(8,128)(2,1)S(1)}, u32[]{:S(2)}, u32[]{:S(2)}) collective-permute-start(bf16[2,128,256]{2,1,0:T(8,128)(2,1)S(1)} %get-tuple-element.39), channel_id=1, source_target_pairs={{1,0},{2,1},{3,2},{4,3},{5,4},{6,5},{7,6},{8,7},{9,8},{10,9},{11,1... | collective-permute-start | bytes 393224 | tf_op jit(solution)/shard_map/ppermute | solution.py:361
  71.0 6.0 %collective-permute-start.4 = (bf16[16,32,720]{2,1,0:T(8,128)(2,1)S(1)}, bf16[16,32,720]{2,1,0:T(8,128)(2,1)S(1)}, u32[]{:S(2)}, u32[]{:S(2)}) collective-permute-start(bf16[16,32,720]{2,1,0:T(8,128)(2,1)S(1)} %get-tuple-element.40), channel_id=1, source_target_pairs={{0,1},{1,0},{2,3},{3,2},{4,5},{5,4},{6,7},{7,6},{8,9},{9,8},{10,11... | collective-permute-start | bytes 2211848 | tf_op jit(solution)/shard_map/ppermute | solution.py:236

commit v6 on v5

--- a/solution.py
+++ b/solution.py
@@ -59,8 +59,7 @@
     return total
 
 
-def first_kernel(tokens_ref, mine_ref, packed_ref, linear_ref):
-    pack(tokens_ref, packed_ref)
+def first_kernel(packed_ref, mine_ref, linear_ref):
     linear_ref[...] = half_linear(packed_ref, mine_ref)
 
 
@@ -296,15 +295,18 @@
     order = (source[:, None] == jnp.arange(KEYF, dtype=jnp.int32)[None, :]).astype(bf16)
 
     other = exchanged(mine, "core")
-    packed, linear = pl.pallas_call(
+    packed = pl.pallas_call(
+        pack,
+        out_shape=jax.ShapeDtypeStruct((parts, rows, dim // parts), bf16),
+        compiler_params=room(8),
+        name="pack",
+    )(tokens)
+    linear = pl.pallas_call(
         first_kernel,
-        out_shape=[
-            jax.ShapeDtypeStruct((parts, rows, dim // parts), bf16),
-            jax.ShapeDtypeStruct((rows, KEYF // 2), f32),
-        ],
+        out_shape=jax.ShapeDtypeStruct((rows, KEYF // 2), f32),
         compiler_params=room(16),
         name="project_own",
-    )(tokens, mine)
+    )(packed, mine)
     keys, edge = pl.pallas_call(
         project_kernel,
         out_shape=[jax.ShapeDtypeStruct((rows, KEYF), bf16), jax.ShapeDtypeStruct((WINDOW, KEYF), bf16)],

time: 129 us -> 133 us (1.031)
  Pallas kernels: 15 us -> 18.1 us
  local copies, waits for them, and re-layouts: 2.3 us -> 4.46 us
    all_to_all x1, waiting for transfers between devices: 12.4 us -> 10.5 us  [spread(): lax.all_to_all(jnp.broadcast_to(x[None], (peers,) + x.shape), axes, 0, 0,...]
    pallas_call x1, Pallas kernels: 0.9 us -> 2.66 us  [per_device(): pl.pallas_call(project_kernel, out_shape=[jax.ShapeDtypeStruct((rows, KEY...]
    unnamed x6 -> x10, local copies, waits for them, and re-layouts: 0.01 us -> 1.55 us
  transfers between devices with their start and end apart: 6 -> 6, of which waited for: 3 -> 3; matrix products, arithmetic and copies ran while one was open for 1% -> 1% of each run, Pallas kernels for 6% -> 8%
where the time goes in v6:
time: 133 us
  blocking collectives  76.9 us (58%)
  Pallas kernels  18.1 us (14%)
  starting transfers between devices  18 us (14%)
  waiting for transfers between devices  12.6 us (9%)
  local copies, waits for them, and re-layouts  4.46 us (3%)
  other arithmetic  1.68 us (1%)
    all_to_all x2, blocking collectives, summed(): lax.all_to_all(x, axes, 0, 0, tiled=True).astype(f32)  49.8 us
    all_to_all x1, blocking collectives, spread(): lax.all_to_all(jnp.broadcast_to(x[None], (peers,) + x.shape), axes, 0, 0,...  27.2 us
    all_to_all x1, waiting for transfers between devices, spread(): lax.all_to_all(jnp.broadcast_to(x[None], (peers,) + x.shape), axes, 0, 0,...  10.5 us
    all_to_all x1, starting transfers between devices, spread(): lax.all_to_all(jnp.broadcast_to(x[None], (peers,) + x.shape), axes, 0, 0,...  7.03 us
    pallas_call x1, Pallas kernels, per_device(): pl.pallas_call(early_kernel, grid=(KV_HEADS // 2,), in_specs=[heads(WINDO...  6 us
    ppermute x2, starting transfers between devices, exchanged(): return lax.ppermute(x, axis, [(0, 1), (1, 0)])  5.78 us
    pallas_call x1, Pallas kernels, per_device(): pl.pallas_call(late_kernel, grid=(KV_HEADS // 2,), in_specs=[heads(ROWS,...  4.09 us
    pallas_call x1, Pallas kernels, per_device(): pl.pallas_call(input_kernel, out_shape=[jax.ShapeDtypeStruct((rows, dim),...  3.22 us
  transfers between devices with their start and end apart: 6, of which 3 were waited for; matrix products, arithmetic and copies ran while one was open for 1% of the time, Pallas kernels for 8%

profile of v6, /device:TPU:32, one launch (start us, length us, event | category | flops | bytes accessed | tf_op | source)
XLA Modules:
  0.0 132.6 jit_solution(7692032727432737497)
XLA Ops:
  0.6 0.0 copy-start.1
  0.6 0.0 copy-start
  0.7 0.8 broadcast_in_dim.20
  1.4 27.2 %all_to_all.20 = bf16[16,8,180]{2,1,0:T(8,128)(2,1)S(1)} all-to-all(bf16[16,8,180]{2,1,0:T(8,128)(2,1)S(1)} %broadcast_in_dim.20), channel_id=1, replica_groups=mesh['zl'=4,'y'=4,'zh'=4,'x'=4,'core'=2] {'zl','zh'}, dimensions={0} | all-to-all | bytes 92160 | tf_op jit(solution)/shard_map/all_to_all | solution.py:231
  28.6 0.1 copy.13
  28.6 0.1 broadcast_in_dim.21
  28.8 1.0 broadcast_in_dim.40
  29.7 7.0 %all-to-all-start.1 = ((bf16[16,32,720]{2,1,0:T(8,128)(2,1)}), bf16[16,32,720]{2,1,0:T(8,128)(2,1)S(1)}, u32[]{:S(2)}, u32[]{:S(2)}) async-start(bf16[16,32,720]{2,1,0:T(8,128)(2,1)} %broadcast_in_dim.40), calls=%async_computation.1 | async-start | bytes 1572864 | tf_op jit(solution)/shard_map/all_to_all | solution.py:231
  36.8 0.0 copy-done.1
  36.8 0.0 copy-start.4
  36.8 0.6 slice_bitcast_fusion
  37.4 1.9 %collective-permute-start.2 = (bf16[128,256]{1,0:T(8,128)(2,1)}, bf16[128,256]{1,0:T(8,128)(2,1)}, u32[]{:S(2)}, u32[]{:S(2)}) collective-permute-start(bf16[128,256]{1,0:T(8,128)(2,1)} %slice_bitcast_fusion), channel_id=1, source_target_pairs={{0,1},{1,2},{2,3},{3,4},{4,5},{5,6},{6,7},{7,8},{8,9},{9,10},{10,1... | collective-permute-start | bytes 196616 | tf_op jit(solution)/shard_map/ppermute | solution.py:270
  39.3 0.0 copy-done
  39.3 0.6 pack.1.packed_ref
  40.0 10.5 %all-to-all-done.1.mine_ref = bf16[16,32,720]{2,1,0:T(8,128)(2,1)S(1)} async-done(((bf16[16,32,720]{2,1,0:T(8,128)(2,1)}), bf16[16,32,720]{2,1,0:T(8,128)(2,1)S(1)}, u32[]{:S(2)}, u32[]{:S(2)}) %all-to-all-start.1) | async-done | bytes 737312 | tf_op jit(solution)/shard_map/all_to_all | solution.py:231
  50.5 0.0 copy-done.4
  50.5 0.1 pad_dynamic-slice_fusion
  50.6 1.9 %collective-permute-start = (bf16[16,32,720]{2,1,0:T(8,128)(2,1)S(1)}, bf16[16,32,720]{2,1,0:T(8,128)(2,1)}, u32[]{:S(2)}, u32[]{:S(2)}) collective-permute-start(bf16[16,32,720]{2,1,0:T(8,128)(2,1)S(1)} %all-to-all-done.1.mine_ref), channel_id=1, source_target_pairs={{0,1},{1,0},{2,3},{3,2},{4,5},{5,4},{6,7},{7,6},{8,9},{9,8},{10,11... | collective-permute-start | bytes 2211848 | tf_op jit(solution)/shard_map/ppermute | solution.py:235
  52.5 0.2 convert_reduce_fusion
  52.7 0.1 reduce_sum.33
  52.8 0.5 project_own.1.linear_ref
  53.3 0.1 fusion.order_ref
  53.4 0.4 fusion.1
  53.8 1.1 collective-permute-done.other_ref
  54.9 2.7 %project.1 = (bf16[192,256]{1,0:T(8,128)(2,1)S(1)}, bf16[128,256]{1,0:T(8,128)(2,1)}) custom-call(bf16[4,192,720]{2,1,0:T(8,128)(2,1)S(1)} %pack.1.packed_ref, bf16[16,32,720]{2,1,0:T(8,128)(2,1)} %collective-permute-done.other_ref, f32[192,128]{1,0:T(8,128)S(1)} %project_own.1.linear_ref, bf16[256,256]{1,0:T(8,128)(2,1)S(1)} %fusion.order_ref, ...), custom_call_target="tpu_custom_call" | custom-call | tf_op jit(solution)/shard_map/project/pallas_call | solution.py:310
  57.6 0.0 copy-start.2
  57.6 0.6 copy-done.2
  58.2 2.0 %collective-permute-start.1 = (bf16[128,256]{1,0:T(8,128)(2,1)}, bf16[128,256]{1,0:T(8,128)(2,1)S(1)}, u32[]{:S(2)}, u32[]{:S(2)}) collective-permute-start(bf16[128,256]{1,0:T(8,128)(2,1)} %get-tuple-element.30), channel_id=1, source_target_pairs={{0,1},{1,2},{2,3},{3,4},{4,5},{5,6},{6,7},{7,8},{8,9},{9,10},{10,1... | collective-permute-start | bytes 196616 | tf_op jit(solution)/shard_map/ppermute | solution.py:317
  60.3 0.1 tile.9.low_ref
  60.4 0.0 collective-permute-done.2.prior_v_ref
  60.4 1.0 collective-permute-done.1.prior_k_ref
  61.3 0.0 copy-start.3
  61.3 0.9 copy-done.3
  62.2 6.0 %band_early.1 = (bf16[192,2048]{1,0:T(8,128)(2,1)}, f32[128,256]{1,0:T(8,128)S(1)}, f32[128,256]{1,0:T(8,128)S(1)}, bf16[2,128,256]{2,1,0:T(8,128)(2,1)S(1)}) custom-call(bf16[192,2048]{1,0:T(8,128)(2,1)} %bitcast.21, bf16[192,2048]{1,0:T(8,128)(2,1)} %bitcast.23, bf16[192,256]{1,0:T(8,128)(2,1)S(1)} %copy-done.3, bf16[192,256]{1,0:T(8,128)(2,1)S(1)} %bitcast.19, ...), custom_call_target="tpu_custom_call" | custom-call | tf_op jit(solution)/shard_map/band_early/pallas_call | solution.py:339
  68.2 1.3 collective-permute-start.3
  69.5 4.1 %band_late.1 = (bf16[192,2048]{1,0:T(8,128)(2,1)}, f32[192,256]{1,0:T(8,128)S(1)}, f32[192,256]{1,0:T(8,128)S(1)}) custom-call(bf16[192,2048]{1,0:T(8,128)(2,1)} %bitcast.22, bf16[192,2048]{1,0:T(8,128)(2,1)} %bitcast.24, bf16[192,256]{1,0:T(8,128)(2,1)S(1)} %copy-done.3, bf16[192,256]{1,0:T(8,128)(2,1)S(1)} %bitcast.20, ...), custom_call_target="tpu_custom_call", output_to_operand_aliasing={{0}: (5, {})} | custom-call | tf_op jit(solution)/shard_map/band_late/pallas_call | solution.py:365
  73.6 0.0 collective-permute-done.3.edge_ref
  73.6 1.0 tail.1
  74.7 3.9 %collective-permute-start.4 = (bf16[16,32,720]{2,1,0:T(8,128)(2,1)S(1)}, bf16[16,32,720]{2,1,0:T(8,128)(2,1)S(1)}, u32[]{:S(2)}, u32[]{:S(2)}) collective-permute-start(bf16[16,32,720]{2,1,0:T(8,128)(2,1)S(1)} %get-tuple-element.36), channel_id=1, source_target_pairs={{0,1},{1,0},{2,3},{3,2},{4,5},{5,4},{6,7},{7,6},{8,9},{9,8},{10,11... | collective-permute-start | bytes 2211848 | tf_op jit(solution)/shard_map/ppermute | solution.py:235
  78.5 3.2 %input_grad.1 = (bf16[192,2880]{1,0:T(8,128)(2,1)}, bf16[192,256]{1,0:T(8,128)(2,1)}) custom-call(bf16[192,256]{1,0:T(8,128)(2,1)S(1)} %get-tuple-element.37.lin_ref, bf16[256,256]{1,0:T(8,128)(2,1)S(1)} %fusion.order_ref, bf16[16,32,720]{2,1,0:T(8,128)(2,1)S(1)} %all-to-all-done.1.mine_ref, bf16[16,32,720]{2,1,0:T(8,128)(2,1)} %collective-permute-done.other_ref, ...), custom_call_target="tpu_custom_call" | custom-call | tf_op jit(solution)/shard_map/input_grad/pallas_call | solution.py:399
  81.8 0.0 collective-permute-done.4
  81.8 0.2 add_convert_fusion
  82.0 27.4 %all_to_all.21 = bf16[16,32,720]{2,1,0:T(8,128)(2,1)S(1)} all-to-all(bf16[16,32,720]{2,1,0:T(8,128)(2,1)S(1)} %add_convert_fusion), channel_id=1, replica_groups=mesh['zl'=4,'y'=4,'zh'=4,'x'=4,'core'=2] {'y','x'}, dimensions={0} | all-to-all | bytes 1474560 | tf_op jit(solution)/shard_map/all_to_all | solution.py:246
  109.3 0.1 reduce_sum.34
  109.4 0.1 reshape.168
  109.6 22.4 %all_to_all.22 = bf16[16,8,180]{2,1,0:T(8,128)(2,1)S(1)} all-to-all(bf16[16,8,180]{2,1,0:T(8,128)(2,1)S(1)} %bitcast.28), channel_id=1, replica_groups=mesh['zl'=4,'y'=4,'zh'=4,'x'=4,'core'=2] {'zl','zh'}, dimensions={0} | all-to-all | bytes 92160 | tf_op jit(solution)/shard_map/all_to_all | solution.py:246
  132.0 0.6 convert_reduce_fusion.1
  (7 shorter events, 0.1 us)
Async XLA Ops:
  0.6 36.1 %copy-start.1 = (bf16[1,192,256]{2,1,0:T(8,128)(2,1)S(1)}, bf16[1,192,256]{2,1,0:T(8,128)(2,1)}, u32[]{:S(2)}) copy-start(bf16[1,192,256]{2,1,0:T(8,128)(2,1)} %param.8) | copy-start | bytes 294916
  0.6 38.7 %copy-start = (bf16[1,192,2880]{2,1,0:T(8,128)(2,1)S(1)}, bf16[1,192,2880]{2,1,0:T(8,128)(2,1)}, u32[]{:S(2)}) copy-start(bf16[1,192,2880]{2,1,0:T(8,128)(2,1)} %param.6) | copy-start | bytes 3317764
  29.7 20.8 %all-to-all-start.1 = ((bf16[16,32,720]{2,1,0:T(8,128)(2,1)}), bf16[16,32,720]{2,1,0:T(8,128)(2,1)S(1)}, u32[]{:S(2)}, u32[]{:S(2)}) async-start(bf16[16,32,720]{2,1,0:T(8,128)(2,1)} %broadcast_in_dim.40), calls=%async_computation.1 | async-start | bytes 1572864 | tf_op jit(solution)/shard_map/all_to_all | solution.py:231
  36.8 13.7 %copy-start.4 = (s32[1,6144]{1,0:T(1,128)S(1)}, s32[1,6144]{1,0:T(1,128)}, u32[]{:S(2)}) copy-start(s32[1,6144]{1,0:T(1,128)} %param.11) | copy-start | bytes 73732
  37.4 22.9 %collective-permute-start.2 = (bf16[128,256]{1,0:T(8,128)(2,1)}, bf16[128,256]{1,0:T(8,128)(2,1)}, u32[]{:S(2)}, u32[]{:S(2)}) collective-permute-start(bf16[128,256]{1,0:T(8,128)(2,1)} %slice_bitcast_fusion), channel_id=1, source_target_pairs={{0,1},{1,2},{2,3},{3,4},{4,5},{5,6},{6,7},{7,8},{8,9},{9,10},{10,1... | collective-permute-start | bytes 196616 | tf_op jit(solution)/shard_map/ppermute | solution.py:270
  50.6 4.3 %collective-permute-start = (bf16[16,32,720]{2,1,0:T(8,128)(2,1)S(1)}, bf16[16,32,720]{2,1,0:T(8,128)(2,1)}, u32[]{:S(2)}, u32[]{:S(2)}) collective-permute-start(bf16[16,32,720]{2,1,0:T(8,128)(2,1)S(1)} %all-to-all-done.1.mine_ref), channel_id=1, source_target_pairs={{0,1},{1,0},{2,3},{3,2},{4,5},{5,4},{6,7},{7,6},{8,9},{9,8},{10,11... | collective-permute-start | bytes 2211848 | tf_op jit(solution)/shard_map/ppermute | solution.py:235
  57.6 0.6 copy-start.2
  58.2 3.1 %collective-permute-start.1 = (bf16[128,256]{1,0:T(8,128)(2,1)}, bf16[128,256]{1,0:T(8,128)(2,1)S(1)}, u32[]{:S(2)}, u32[]{:S(2)}) collective-permute-start(bf16[128,256]{1,0:T(8,128)(2,1)} %get-tuple-element.30), channel_id=1, source_target_pairs={{0,1},{1,2},{2,3},{3,4},{4,5},{5,6},{6,7},{7,8},{8,9},{9,10},{10,1... | collective-permute-start | bytes 196616 | tf_op jit(solution)/shard_map/ppermute | solution.py:317
  61.3 0.9 copy-start.3
  68.2 5.4 %collective-permute-start.3 = (bf16[2,128,256]{2,1,0:T(8,128)(2,1)S(1)}, bf16[2,128,256]{2,1,0:T(8,128)(2,1)S(1)}, u32[]{:S(2)}, u32[]{:S(2)}) collective-permute-start(bf16[2,128,256]{2,1,0:T(8,128)(2,1)S(1)} %get-tuple-element.35), channel_id=1, source_target_pairs={{1,0},{2,1},{3,2},{4,3},{5,4},{6,5},{7,6},{8,7},{9,8},{10,9},{11,1... | collective-permute-start | bytes 393224 | tf_op jit(solution)/shard_map/ppermute | solution.py:363
  74.7 7.1 %collective-permute-start.4 = (bf16[16,32,720]{2,1,0:T(8,128)(2,1)S(1)}, bf16[16,32,720]{2,1,0:T(8,128)(2,1)S(1)}, u32[]{:S(2)}, u32[]{:S(2)}) collective-permute-start(bf16[16,32,720]{2,1,0:T(8,128)(2,1)S(1)} %get-tuple-element.36), channel_id=1, source_target_pairs={{0,1},{1,0},{2,3},{3,2},{4,5},{5,4},{6,7},{7,6},{8,9},{9,8},{10,11... | collective-permute-start | bytes 2211848 | tf_op jit(solution)/shard_map/ppermute | solution.py:235
